TPU v7x, 32 devices: a whole 2x2x4 slice. The times are simulated.
32 devices in a mesh: grp: 2 (over y), seq: 8 (over z, x), tp: 2 (over core).
Axes of the slice: x: 2, y: 2, z: 4, core: 2. Of those that a mesh axis runs over, the one named last changes fastest.
Arguments:
- queries: bfloat16 [4096, 2048], P(('grp', 'seq'), 'tp'), parts along dimension 0, may hold values from -9 to 9
- keys: bfloat16 [4096, 2048], P(('grp', 'seq'), 'tp'), parts along dimension 0, may hold values from -9 to 9
- values: bfloat16 [4096, 2048], P(('grp', 'seq'), 'tp'), parts along dimension 0, may hold values from -18 to 18
- segment_ids: int32 [4096], P(('grp', 'seq')), parts along dimension 0, may hold values from 0 to 7, never falling along the last dimension, each value on 1 to 512 neighbouring positions
- modality: int32 [4096], P(('grp', 'seq')), parts along dimension 0, may hold values 0 or 1
- norm_gain: float32 [2, 2048], P(None, 'tp'), may hold values from 0.1 to 1.9
Outputs:
- blended: bfloat16 [4096, 2048], P(('grp', 'seq'), 'tp'), parts along dimension 0
There are 2 independent parts, one for each index of `grp`. A program takes and returns all parts, laid end to end along the dimension named above; an argument that names none is the same for every part. Nothing has to cross between parts.
Inputs may be any that keep to these rules, and one draw needn't show every extreme that they name: `segment_ids`: ids never fall along the sequence; each document holds 1 to 512 tokens, and one holds exactly that many.
All inputs are finite; a program needn't handle non-finite values. No bound on the sum of `modality` on one device may be relied on, other than what follows from the above.
Results may differ from a plain program's by a relative error of at most 0.009.
Values may be sent and summed in bfloat16 or wider, within the bound.
No kernel may reach another device: no remote copies, remote signals or barrier semaphores. Data moves between devices by JAX's collectives and lax.ppermute only.
A program may use at most 64 MiB of HBM per device.

v0:
```python
import jax
import jax.numpy as jnp
from jax import lax
from jax.sharding import PartitionSpec as P

HEADS = 16
HEAD_DIM = 128
REACH = 2


def shifted(value, axis, steps):
    count = lax.axis_size(axis)
    initial, last = (max(0, -steps), min(count, count - steps))
    return lax.ppermute(value, axis, [(source, source + steps) for source in range(initial, last)])


def on_device(queries, keys, values, segment_ids, modality, norm_gain):
    tok_rows, feat_width = queries.shape
    head_count = feat_width // HEAD_DIM
    my_index = lax.axis_index("seq")
    score_scale = HEAD_DIM ** (-0.5)
    query_heads = queries.reshape(tok_rows, head_count, HEAD_DIM)
    offsets = jnp.arange(tok_rows, dtype=jnp.int32)
    query_pos = my_index * tok_rows + offsets

    def absorb(running, key_block, value_block, key_segs, distance):
        run_max, run_total, run_acc = running
        scores = (
            jnp.einsum(
                "qhd,khd->hqk",
                query_heads,
                key_block.reshape(tok_rows, head_count, HEAD_DIM),
                preferred_element_type=jnp.float32,
            )
            * score_scale
        )
        key_pos = (my_index - distance) * tok_rows + offsets
        allowed = (
            (segment_ids[:, None] == key_segs[None, :])
            & (key_pos[None, :] <= query_pos[:, None])
            & (my_index >= distance)
        )
        scores = jnp.where(allowed[None], scores, -jnp.inf)
        new_max = jnp.maximum(run_max, jnp.max(scores, axis=2))
        weights = jnp.exp(scores - new_max[:, :, None])
        factor = jnp.exp(run_max - new_max)
        new_total = run_total * factor + jnp.sum(weights, axis=2)
        contrib = jnp.einsum(
            "hqk,khd->hqd",
            weights.astype(jnp.bfloat16),
            value_block.reshape(tok_rows, head_count, HEAD_DIM),
            preferred_element_type=jnp.float32,
        )
        return (new_max, new_total, run_acc * factor[:, :, None] + contrib)

    start_state = (
        jnp.full((head_count, tok_rows), -jnp.inf, jnp.float32),
        jnp.zeros((head_count, tok_rows), jnp.float32),
        jnp.zeros((head_count, tok_rows, HEAD_DIM), jnp.float32),
    )
    running = absorb(start_state, keys, values, segment_ids, 0)
    for distance in range(1, REACH + 1):
        arrived = shifted((keys, values, segment_ids), "seq", distance)
        running = absorb(running, arrived[0], arrived[1], arrived[2], distance)
    run_max, run_total, run_acc = running
    attended = (run_acc / run_total[:, :, None]).astype(jnp.bfloat16)
    attended = jnp.transpose(attended, (1, 0, 2)).reshape(tok_rows, feat_width).astype(jnp.float32)
    partial_value = jnp.sum(attended * attended, axis=1)
    total = lax.psum(partial_value, "tp")
    mean_square = total / (HEADS * HEAD_DIM)
    gain_rows = jnp.where((modality == 1)[:, None], norm_gain[1][None, :], norm_gain[0][None, :])
    blended = attended * lax.rsqrt(mean_square + 1e-05)[:, None] * gain_rows
    return blended.astype(jnp.bfloat16)


def solution(mesh):
    return jax.shard_map(
        on_device,
        mesh=mesh,
        in_specs=(
            P(("grp", "seq"), "tp"),
            P(("grp", "seq"), "tp"),
            P(("grp", "seq"), "tp"),
            P(("grp", "seq")),
            P(("grp", "seq")),
            P(None, "tp"),
        ),
        out_specs=P(("grp", "seq"), "tp"),
        check_vma=False,
    )
```

profile of v0, /device:TPU:11, one launch (start us, length us, event | category | flops | bytes accessed | tf_op | source)
XLA Modules:
  0.0 65.1 jit_solution(13082774962858657751)
XLA Ops:
  0.0 0.0 copy-start
  0.0 0.0 copy-start.4
  0.0 0.0 copy-start.3
  0.0 3.3 %collective-permute-start = (s32[256]{0:T(256)}, s32[256]{0:T(256)S(1)}, u32[]{:S(2)}, u32[]{:S(2)}) collective-permute-start(s32[256]{0:T(256)} %param.9), channel_id=1, source_target_pairs={{0,2},{2,4},{4,6},{6,8},{8,10},{10,12},{12,14},{1,3},{3,5},{5,7},{... | collective-permute-start | bytes 3080 | tf_op jit(solution)/shard_map/ppermute | solution.py:14
  3.3 3.2 %collective-permute-start.3 = (s32[256]{0:T(256)}, s32[256]{0:T(256)S(1)}, u32[]{:S(2)}, u32[]{:S(2)}) collective-permute-start(s32[256]{0:T(256)} %param.9), channel_id=1, source_target_pairs={{0,4},{2,6},{4,8},{6,10},{8,12},{10,14},{1,5},{3,7},{5,9},{7,11},{... | collective-permute-start | bytes 3080 | tf_op jit(solution)/shard_map/ppermute | solution.py:14
  6.5 1.2 %copy.22 = bf16[256,1024]{0,1:T(8,128)(2,1)S(1)} copy(bf16[256,1024]{1,0:T(8,128)(2,1)} %param.7) | data formatting | bytes 1048576 | tf_op args[1]
  7.8 1.9 %collective-permute-start.4 = (bf16[256,1024]{0,1:T(8,128)(2,1)S(1)}, bf16[256,1024]{0,1:T(8,128)(2,1)S(1)}, u32[]{:S(2)}, u32[]{:S(2)}) collective-permute-start(bf16[256,1024]{0,1:T(8,128)(2,1)S(1)} %copy.22), channel_id=1, source_target_pairs={{0,4},{2,6},{4,8},{6,10},{8,12},{10,14},{1,5},{3,7},{5,9},{7,11},{... | collective-permute-start | bytes 1572872 | tf_op jit(solution)/shard_map/ppermute | solution.py:14
  9.7 3.1 %collective-permute-start.1 = (bf16[256,1024]{0,1:T(8,128)(2,1)S(1)}, bf16[256,1024]{0,1:T(8,128)(2,1)S(1)}, u32[]{:S(2)}, u32[]{:S(2)}) collective-permute-start(bf16[256,1024]{0,1:T(8,128)(2,1)S(1)} %copy.22), channel_id=1, source_target_pairs={{0,2},{2,4},{4,6},{6,8},{8,10},{10,12},{12,14},{1,3},{3,5},{5,7},{... | collective-permute-start | bytes 1572872 | tf_op jit(solution)/shard_map/ppermute | solution.py:14
  12.8 1.9 %collective-permute-start.2 = (bf16[256,1024]{1,0:T(8,128)(2,1)}, bf16[256,1024]{1,0:T(8,128)(2,1)}, u32[]{:S(2)}, u32[]{:S(2)}) collective-permute-start(bf16[256,1024]{1,0:T(8,128)(2,1)} %param.8), channel_id=1, source_target_pairs={{0,2},{2,4},{4,6},{6,8},{8,10},{10,12},{12,14},{1,3},{3,5},{5,7},{... | collective-permute-start | bytes 1572872 | tf_op jit(solution)/shard_map/ppermute | solution.py:14
  14.8 0.8 %fusion.58 = (f32[1,1024]{1,0:T(1,128)S(1)}, f32[1,1024]{1,0:T(1,128)S(1)}) fusion(f32[2,1024]{1,0:T(2,128)} %param.11), kind=kLoop, calls=%fused_computation.79 | loop fusion | bytes 16384 | tf_op jit(solution)/shard_map/slice | solution.py:71
  15.6 0.7 %broadcast_compare_fusion = pred[256]{0:T(512)(128)(4,1)S(1)} fusion(s32[256]{0:T(256)} %param.10), kind=kLoop, calls=%fused_computation.71 | loop fusion | flops 256 | bytes 1280 | tf_op jit(solution)/shard_map/eq | solution.py:71
  16.3 2.0 %copy.38 = bf16[256,1024]{0,1:T(8,128)(2,1)} copy(bf16[256,1024]{1,0:T(8,128)(2,1)} %param.8) | data formatting | bytes 1048576 | tf_op jit(solution)/shard_map/reshape | solution.py:51
  18.3 0.0 collective-permute-done
  18.3 1.9 %collective-permute-start.5 = (bf16[256,1024]{1,0:T(8,128)(2,1)}, bf16[256,1024]{1,0:T(8,128)(2,1)}, u32[]{:S(2)}, u32[]{:S(2)}) collective-permute-start(bf16[256,1024]{1,0:T(8,128)(2,1)} %param.8), channel_id=1, source_target_pairs={{0,4},{2,6},{4,8},{6,10},{8,12},{10,14},{1,5},{3,7},{5,9},{7,11},{... | collective-permute-start | bytes 1572872 | tf_op jit(solution)/shard_map/ppermute | solution.py:14
  20.2 0.0 collective-permute-done.3
  20.3 0.0 copy-done.4
  20.3 0.3 and_and_fusion.1
  20.6 0.0 copy-done
  20.6 0.0 copy-done.3
  20.6 0.5 fusion
  21.1 0.0 copy-start.2
  21.1 0.9 %collective-permute-done.4 = bf16[256,1024]{0,1:T(8,128)(2,1)S(1)} collective-permute-done((bf16[256,1024]{0,1:T(8,128)(2,1)S(1)}, bf16[256,1024]{0,1:T(8,128)(2,1)S(1)}, u32[]{:S(2)}, u32[]{:S(2)}) %collective-permute-start.4) | collective-permute-done | bytes 524320 | tf_op jit(solution)/shard_map/ppermute | solution.py:14
  21.9 0.5 fusion.2
  22.5 0.0 copy-start.1
  22.5 8.8 %collective-permute-done.1 = bf16[256,1024]{0,1:T(8,128)(2,1)S(1)} collective-permute-done((bf16[256,1024]{0,1:T(8,128)(2,1)S(1)}, bf16[256,1024]{0,1:T(8,128)(2,1)S(1)}, u32[]{:S(2)}, u32[]{:S(2)}) %collective-permute-start.1) | collective-permute-done | bytes 524320 | tf_op jit(solution)/shard_map/ppermute | solution.py:14
  31.3 0.6 fusion.1
  31.8 0.0 copy-done.2
  31.8 0.9 %fusion.3 = (f32[8,256]{1,0:T(8,128)S(1)}, f32[8,256]{1,0:T(8,128)S(1)}) fusion(f32[8,256,256]{1,2,0:T(8,128)S(1)} %get-tuple-element.17, f32[8,256]{1,0:T(8,128)S(1)} %get-tuple-element.16, pred[256,256]{0,1:T(8,128)(4,1)S(1)} %get-tuple-element.15, f32[8,256]{1,0:T(8,128)S(1)} %get-tuple-element.9, f32[8,256,256]{1,2,0:T(8,128)S(1)} %get-tuple-element.21, ...), kind=kLoop, calls=%fused_computation.9 | loop fusion | flops 4190208 | bytes 4358144 | tf_op jit(solution)/shard_map/reduce_sum | solution.py:47
  32.7 0.0 copy-done.1
  32.8 0.4 fusion.7
  33.2 9.4 %collective-permute-done.2 = bf16[256,1024]{1,0:T(8,128)(2,1)} collective-permute-done((bf16[256,1024]{1,0:T(8,128)(2,1)}, bf16[256,1024]{1,0:T(8,128)(2,1)}, u32[]{:S(2)}, u32[]{:S(2)}) %collective-permute-start.2) | collective-permute-done | bytes 524320 | tf_op jit(solution)/shard_map/ppermute | solution.py:14
  42.6 1.2 %copy.25 = bf16[256,1024]{0,1:T(8,128)(2,1)S(1)} copy(bf16[256,1024]{1,0:T(8,128)(2,1)} %collective-permute-done.2) | data formatting | bytes 1048576 | tf_op jit(solution)/shard_map/ppermute | solution.py:14
  43.8 2.4 %fusion.14 = f32[256,8,128]{0,2,1:T(8,128)S(1)} fusion(bf16[256,8,128]{0,2,1:T(8,128)(2,1)} %bitcast.114, f32[8,256,256]{1,2,0:T(8,128)} %copy-done.2, f32[8,256]{1,0:T(8,128)S(1)} %get-tuple-element.16, pred[256,256]{0,1:T(8,128)(4,1)S(1)} %get-tuple-element.15, f32[256,8]{0,1:T(8,128)S(1)} %get-tuple-element.7, f32[256,8]{0,1:T(8,128)S(1)} %get-tuple-element.12), kind=kOutput, calls=%fused_computation.23 | convolution fusion | flops 136839168 | bytes 3760128 | tf_op jit(solution)/shard_map/hqk,khd->hqd/dot_general | solution.py:48
  46.3 1.7 %fusion.12 = f32[256,8,128]{0,2,1:T(8,128)} fusion(f32[256,8,128]{0,2,1:T(8,128)S(1)} %fusion.14, bf16[256,8,128]{0,2,1:T(8,128)(2,1)S(1)} %bitcast.110, f32[8,256,256]{1,2,0:T(8,128)S(1)} %get-tuple-element.21, f32[8,256]{1,0:T(8,128)S(1)} %get-tuple-element.9, pred[256,256]{0,1:T(8,128)(4,1)S(1)} %get-tuple-element.13, f32[256,8]{0,1:T(8,128)S(1)} %get-tuple-element.6), kind=kOutput, calls=%fused_computation.20 | convolution fusion | flops 136839168 | bytes 4800512 | tf_op jit(solution)/shard_map/hqk,khd->hqd/dot_general | solution.py:48
  47.9 7.8 %collective-permute-done.5 = bf16[256,1024]{1,0:T(8,128)(2,1)} collective-permute-done((bf16[256,1024]{1,0:T(8,128)(2,1)}, bf16[256,1024]{1,0:T(8,128)(2,1)}, u32[]{:S(2)}, u32[]{:S(2)}) %collective-permute-start.5) | collective-permute-done | bytes 524320 | tf_op jit(solution)/shard_map/ppermute | solution.py:14
  55.7 1.2 %copy.30 = bf16[256,1024]{0,1:T(8,128)(2,1)S(1)} copy(bf16[256,1024]{1,0:T(8,128)(2,1)} %collective-permute-done.5) | data formatting | bytes 1048576 | tf_op jit(solution)/shard_map/ppermute | solution.py:14
  57.0 2.5 %multiply_reduce_fusion = (f32[256]{0:T(256)S(1)}, f32[256,8,128]{0,2,1:T(8,128)S(1)}) fusion(f32[256,8]{0,1:T(8,128)S(1)} %get-tuple-element.5, f32[256,8,128]{0,2,1:T(8,128)} %fusion.12, bf16[256,8,128]{0,2,1:T(8,128)(2,1)S(1)} %bitcast.115, f32[8,256,256]{1,2,0:T(8,128)} %copy-done.1, f32[8,256]{1,0:T(8,128)S(1)} %get-tuple-element.8, ...), kind=kOutput, calls=%fused_computation.27 | convolution fusion | flops 137887488 | bytes 4801536 | tf_op jit(solution)/shard_map/hqk,khd->hqd/dot_general | solution.py:48
  59.5 0.3 copy.32
  59.8 4.2 %psum.7 = f32[256]{0:T(256)S(1)} all-reduce(f32[256]{0:T(256)S(1)} %get-tuple-element.22), channel_id=1, replica_groups=mesh['grp'=2,'seq'=8,'tp'=2] {'tp'}, use_global_device_ids=true, to_apply=%region_7.8 | all-reduce | flops 256 | bytes 2048 | tf_op jit(solution)/shard_map/psum | solution.py:69
  64.1 1.0 %multiply_convert_fusion = bf16[256,1024]{1,0:T(8,128)(2,1)} fusion(f32[256,1024]{1,0:T(8,128)S(1)} %copy.32, f32[1024]{0:T(1024)S(1)} %bitcast.117, f32[1024]{0:T(1024)S(1)} %bitcast.116, f32[256]{0:T(256)S(1)} %add_rsqrt_fusion, pred[256]{0:T(512)(128)(4,1)S(1)} %broadcast_compare_fusion), kind=kLoop, calls=%fused_computation.26 | loop fusion | flops 1048576 | bytes 1582336 | tf_op jit(solution)/shard_map/convert_element_type | solution.py:73
  (6 shorter events, 0.0 us)
Async XLA Ops:
  0.0 20.6 %copy-start = (bf16[256,1024]{1,0:T(8,128)(2,1)S(1)}, bf16[256,1024]{1,0:T(8,128)(2,1)}, u32[]{:S(2)}) copy-start(bf16[256,1024]{1,0:T(8,128)(2,1)} %param.6) | copy-start | bytes 1572868
  0.0 20.3 %copy-start.4 = (s32[256]{0:T(256)S(1)}, s32[256]{0:T(256)}, u32[]{:S(2)}) copy-start(s32[256]{0:T(256)} %param.9) | copy-start | bytes 3076
  0.0 20.6 %copy-start.3 = (bf16[256,1024]{1,0:T(8,128)(2,1)S(1)}, bf16[256,1024]{1,0:T(8,128)(2,1)}, u32[]{:S(2)}) copy-start(bf16[256,1024]{1,0:T(8,128)(2,1)} %param.7) | copy-start | bytes 1572868
  0.0 18.3 %collective-permute-start = (s32[256]{0:T(256)}, s32[256]{0:T(256)S(1)}, u32[]{:S(2)}, u32[]{:S(2)}) collective-permute-start(s32[256]{0:T(256)} %param.9), channel_id=1, source_target_pairs={{0,2},{2,4},{4,6},{6,8},{8,10},{10,12},{12,14},{1,3},{3,5},{5,7},{... | collective-permute-start | bytes 3080 | tf_op jit(solution)/shard_map/ppermute | solution.py:14
  3.3 16.9 %collective-permute-start.3 = (s32[256]{0:T(256)}, s32[256]{0:T(256)S(1)}, u32[]{:S(2)}, u32[]{:S(2)}) collective-permute-start(s32[256]{0:T(256)} %param.9), channel_id=1, source_target_pairs={{0,4},{2,6},{4,8},{6,10},{8,12},{10,14},{1,5},{3,7},{5,9},{7,11},{... | collective-permute-start | bytes 3080 | tf_op jit(solution)/shard_map/ppermute | solution.py:14
  7.8 14.1 %collective-permute-start.4 = (bf16[256,1024]{0,1:T(8,128)(2,1)S(1)}, bf16[256,1024]{0,1:T(8,128)(2,1)S(1)}, u32[]{:S(2)}, u32[]{:S(2)}) collective-permute-start(bf16[256,1024]{0,1:T(8,128)(2,1)S(1)} %copy.22), channel_id=1, source_target_pairs={{0,4},{2,6},{4,8},{6,10},{8,12},{10,14},{1,5},{3,7},{5,9},{7,11},{... | collective-permute-start | bytes 1572872 | tf_op jit(solution)/shard_map/ppermute | solution.py:14
  9.7 21.5 %collective-permute-start.1 = (bf16[256,1024]{0,1:T(8,128)(2,1)S(1)}, bf16[256,1024]{0,1:T(8,128)(2,1)S(1)}, u32[]{:S(2)}, u32[]{:S(2)}) collective-permute-start(bf16[256,1024]{0,1:T(8,128)(2,1)S(1)} %copy.22), channel_id=1, source_target_pairs={{0,2},{2,4},{4,6},{6,8},{8,10},{10,12},{12,14},{1,3},{3,5},{5,7},{... | collective-permute-start | bytes 1572872 | tf_op jit(solution)/shard_map/ppermute | solution.py:14
  12.8 29.8 %collective-permute-start.2 = (bf16[256,1024]{1,0:T(8,128)(2,1)}, bf16[256,1024]{1,0:T(8,128)(2,1)}, u32[]{:S(2)}, u32[]{:S(2)}) collective-permute-start(bf16[256,1024]{1,0:T(8,128)(2,1)} %param.8), channel_id=1, source_target_pairs={{0,2},{2,4},{4,6},{6,8},{8,10},{10,12},{12,14},{1,3},{3,5},{5,7},{... | collective-permute-start | bytes 1572872 | tf_op jit(solution)/shard_map/ppermute | solution.py:14
  18.3 37.4 %collective-permute-start.5 = (bf16[256,1024]{1,0:T(8,128)(2,1)}, bf16[256,1024]{1,0:T(8,128)(2,1)}, u32[]{:S(2)}, u32[]{:S(2)}) collective-permute-start(bf16[256,1024]{1,0:T(8,128)(2,1)} %param.8), channel_id=1, source_target_pairs={{0,4},{2,6},{4,8},{6,10},{8,12},{10,14},{1,5},{3,7},{5,9},{7,11},{... | collective-permute-start | bytes 1572872 | tf_op jit(solution)/shard_map/ppermute | solution.py:14
  21.1 10.8 %copy-start.2 = (f32[8,256,256]{1,2,0:T(8,128)}, f32[8,256,256]{1,2,0:T(8,128)S(1)}, u32[]{:S(2)}) copy-start(f32[8,256,256]{1,2,0:T(8,128)S(1)} %get-tuple-element.17) | copy-start | bytes 6291460
  22.5 10.3 %copy-start.1 = (f32[8,256,256]{1,2,0:T(8,128)}, f32[8,256,256]{1,2,0:T(8,128)S(1)}, u32[]{:S(2)}) copy-start(f32[8,256,256]{1,2,0:T(8,128)S(1)} %get-tuple-element.19) | copy-start | bytes 6291460
where the time goes:
time: 65.6 us; the launch traced here: 65.1 us
  waiting for transfers between devices  26.8 us (41%)
  starting transfers between devices  15.4 us (23%)
  matrix products  8.17 us (12%)
  local copies, waits for them, and re-layouts  6.9 us (11%)
  blocking collectives  4.22 us (6%)
  other arithmetic  3.36 us (5%)
    ppermute x6, waiting for transfers between devices, shifted(): lax.ppermute(value, axis, [(source, source + steps) for source in range(i...  26.8 us
    ppermute x6, starting transfers between devices, shifted(): lax.ppermute(value, axis, [(source, source + steps) for source in range(i...  15.4 us
    dot_general x3, matrix products, absorb(): jnp.einsum('hqk,khd->hqd', weights.astype(jnp.bfloat16), value_block.resh...  6.6 us
    psum x1, blocking collectives, on_device(): total = lax.psum(partial_value, 'tp')  4.22 us
    ppermute x2, local copies, waits for them, and re-layouts, shifted(): lax.ppermute(value, axis, [(source, source + steps) for source in range(i...  2.49 us
    reshape x1, local copies, waits for them, and re-layouts, absorb(): value_block.reshape(tok_rows, head_count, HEAD_DIM)  2.04 us
    dot_general x3, matrix products, absorb(): jnp.einsum('qhd,khd->hqk', query_heads, key_block.reshape(tok_rows, head_...  1.57 us
    reduce_sum x2, other arithmetic, absorb(): new_total = run_total * factor + jnp.sum(weights, axis=2)  1.36 us
  transfers between devices with their start and end apart: 6, of which 4 were waited for; matrix products, arithmetic and copies ran while one was open for 20% of the time, Pallas kernels for 0%

commit v1 on v0

v1 whole, which is shorter than its diff:
```python
import functools
import math

import jax
import jax.numpy as jnp
from jax import lax
from jax.experimental import pallas as pl
from jax.experimental.pallas import tpu as pltpu
from jax.sharding import PartitionSpec as P


HEAD_DIM = 128
CHUNKS = 4
SEG_ROWS = 16
NEG = -1e30
EPS = 1e-05


def column(row):
    return jnp.transpose(jnp.broadcast_to(row, (128, row.shape[1])))


def lanes(col, width):
    return jnp.concatenate([col] * (width // 128), axis=1)


def allowed_masks(me, own_seg, near_seg, far_seg):
    tok = own_seg.shape[1]
    q_seg = lanes(column(own_seg), tok)
    q_pos = lax.broadcasted_iota(jnp.int32, (tok, tok), 0)
    k_pos = lax.broadcasted_iota(jnp.int32, (tok, tok), 1)
    near_seg = jnp.where(me >= 1, near_seg, -1.0)
    far_seg = jnp.where(me >= 2, far_seg, -1.0)
    own = (q_seg == own_seg) & (k_pos <= q_pos)
    return own, q_seg == near_seg, q_seg == far_seg


def attend_head(q, keys, values, masks):
    factor = HEAD_DIM ** (-0.5) * math.log2(math.e)
    scores = []
    for key, mask in zip(keys, masks):
        s = lax.dot_general(q, key, (((1,), (1,)), ((), ())), preferred_element_type=jnp.float32)
        scores.append(jnp.where(mask, s, NEG))
    top = functools.reduce(jnp.maximum, scores)
    top = jnp.max(top, axis=1, keepdims=True) * factor
    weights = [jnp.exp2(s * factor - top) for s in scores]
    total = jnp.sum(functools.reduce(jnp.add, weights), axis=1, keepdims=True)
    acc = sum(
        lax.dot_general(w.astype(jnp.bfloat16), v, (((1,), (0,)), ((), ())), preferred_element_type=jnp.float32)
        for w, v in zip(weights, values)
    )
    return (acc / total).astype(jnp.bfloat16)


def attend_kernel(last, me_ref, *refs):
    q_ref, k_ref, v_ref, seg_ref, near_seg_ref, far_seg_ref = refs[:6]
    me = me_ref[0]
    tok, width = q_ref.shape
    seg = seg_ref[...].astype(jnp.float32)
    near_seg = near_seg_ref[...][0:1, :tok].astype(jnp.float32)
    far_seg = far_seg_ref[...][0:1, :tok].astype(jnp.float32)
    masks = allowed_masks(me, seg, near_seg, far_seg)
    if last:
        s_ref, f_ref, a_ref, p0, p1, p2 = refs[6:12]
        att_ref, sq_ref = refs[12:]
        odd = lax.rem(me, 2) == 1
        near = jnp.where(odd, s_ref[...], f_ref[...])
        far = jnp.where(odd, f_ref[...], a_ref[...])
    else:
        near_ref, far_ref = refs[6:8]
        att_ref, sq_ref = refs[8:]
        near, far = near_ref[:tok, :], far_ref[:tok, :]
    squares = None
    for h in range(width // HEAD_DIM):
        ks = slice(h * HEAD_DIM, (h + 1) * HEAD_DIM)
        vs = slice(width + h * HEAD_DIM, width + (h + 1) * HEAD_DIM)
        att = attend_head(
            q_ref[:, ks], (k_ref[:, ks], near[:, ks], far[:, ks]), (v_ref[:, ks], near[:, vs], far[:, vs]), masks
        )
        att_ref[:, ks] = att
        att = att.astype(jnp.float32)
        squares = att * att if squares is None else squares + att * att
    if last:
        squares = jnp.transpose(squares + p0[...] + p1[...] + p2[...])
        sq_ref[...] = jnp.sum(squares.reshape(squares.shape[0] // 8, 8, tok), axis=0)
    else:
        sq_ref[...] = squares


def finish_kernel(features, mine_ref, other_ref, mod_ref, gain_ref, *refs):
    att_refs, out_ref = refs[:-1], refs[-1]
    total = jnp.sum(mine_ref[...] + other_ref[...], axis=0, keepdims=True)
    inverse = column(lax.rsqrt(total / features + EPS))
    image = column(mod_ref[...].astype(jnp.float32)) == 1.0
    for c, att_ref in enumerate(att_refs):
        width = att_ref.shape[1]
        for b in range(width // 128):
            at = c * width + b * 128
            gain = jnp.where(image, gain_ref[1:2, at : at + 128], gain_ref[0:1, at : at + 128])
            att = att_ref[:, b * 128 : (b + 1) * 128].astype(jnp.float32)
            out_ref[:, at : at + 128] = (att * inverse * gain).astype(jnp.bfloat16)


def on_device(queries, keys, values, segment_ids, modality, norm_gain):
    tok, feat = queries.shape
    n = lax.axis_size("seq")
    me = lax.axis_index("seq")
    odd = (me % 2) == 1
    width = feat // CHUNKS
    ring2 = [(i, (i + 2) % n) for i in range(n)]
    shift2 = [(i, i + 2) for i in range(n - 2)]
    pair = [(i, i ^ 1) for i in range(n)]

    def send(value, pairs):
        return lax.ppermute(value, "seq", pairs)

    seg_row = segment_ids.astype(jnp.bfloat16)
    seg_block = jnp.pad(seg_row[None, :], ((0, SEG_ROWS - 1), (0, 2 * width - tok)))
    chunk = []
    for c in range(CHUNKS):
        cols = slice(c * width, (c + 1) * width)
        chunk.append(jnp.concatenate([keys[:, cols], values[:, cols]], axis=1))
    chunk[0] = jnp.concatenate([chunk[0], seg_block], axis=0)
    a0 = send(chunk[0], ring2)
    s = send(chunk[3], pair)
    a1 = send(chunk[1], ring2)
    a2 = send(chunk[2], ring2)
    x0 = send(jnp.where(odd, a0, chunk[0]), pair)
    f = send(jnp.where(odd, chunk[3], s), ring2)
    x1 = send(jnp.where(odd, a1, chunk[1]), pair)
    a3 = send(chunk[3], shift2)
    x2 = send(jnp.where(odd, a2, chunk[2]), pair)

    seg2d = segment_ids[None, :]
    me1 = me.astype(jnp.int32)[None]
    smem = pl.BlockSpec(memory_space=pltpu.SMEM)
    whole = lambda a: pl.BlockSpec(a.shape, lambda i: (0,) * len(a.shape))
    segs = pl.BlockSpec((SEG_ROWS, 2 * width), lambda i: (tok // SEG_ROWS, 0))
    flops = 3 * 4 * tok * tok * width

    def attend(c, last, rest):
        cols = pl.BlockSpec((tok, width), lambda i: (0, c))
        sq_shape = (8, tok) if last else (tok, 128)
        outs = (jax.ShapeDtypeStruct((tok, width), jnp.bfloat16), jax.ShapeDtypeStruct(sq_shape, jnp.float32))
        return pl.pallas_call(
            functools.partial(attend_kernel, last),
            grid=(1,),
            out_shape=outs,
            out_specs=tuple(whole(o) for o in outs),
            in_specs=[smem, cols, cols, cols, whole(seg2d), segs, segs] + [whole(r) for r in rest],
            name="attend_last" if last else "attend",
            cost_estimate=pl.CostEstimate(flops=flops, bytes_accessed=tok * width * 20, transcendentals=3 * tok * tok * 2),
        )(me1, queries, keys, values, seg2d, x0, a0, *rest)

    att, sq = [], []
    for c, (near, far) in enumerate(((x0, a0), (x1, a1), (x2, a2))):
        o, q = attend(c, False, (near, far))
        att.append(o)
        sq.append(q)
    o, q = attend(3, True, (s, f, a3, *sq))
    att.append(o)
    tp = lax.axis_size("tp")
    other = lax.ppermute(q, "tp", [(i, i ^ 1) for i in range(tp)])
    return pl.pallas_call(
        functools.partial(finish_kernel, float(feat * tp)),
        out_shape=jax.ShapeDtypeStruct((tok, feat), jnp.bfloat16),
        name="finish",
    )(q, other, modality[None, :], norm_gain, *att)


def solution(mesh):
    return jax.shard_map(
        on_device,
        mesh=mesh,
        in_specs=(
            P(("grp", "seq"), "tp"),
            P(("grp", "seq"), "tp"),
            P(("grp", "seq"), "tp"),
            P(("grp", "seq")),
            P(("grp", "seq")),
            P(None, "tp"),
        ),
        out_specs=P(("grp", "seq"), "tp"),
        check_vma=False,
    )
```

time: 65.6 us -> 54.9 us (0.84)
  Pallas kernels: 0 us -> 14.8 us
  matrix products: 8.17 us -> 0 us
  starting transfers between devices: 15.4 us -> 9.45 us
  waiting for transfers between devices: 26.8 us -> 22.3 us
  blocking collectives: 4.22 us -> 0 us
  other arithmetic: 3.36 us -> 0.34 us
    pallas_call x0 -> x5, Pallas kernels: none -> 14.8 us  [the longest x4 12.6 us: attend(): pl.pallas_call(functools.partial(attend_kernel, last), grid=(1,), out_sha...]
    dot_general x6 -> x0, matrix products: 8.17 us -> none  [the longest x3 6.6 us: absorb(): jnp.einsum('hqk,khd->hqd', weights.astype(jnp.bfloat16), value_block.resh...]
    ppermute x6 -> x10, starting transfers between devices: 15.4 us -> 9.45 us  [the longest x9 7.07 us: send(): return lax.ppermute(value, 'seq', pairs)]
    unnamed x11 -> x20, local copies, waits for them, and re-layouts: 1.26 us -> 5.9 us
    ppermute x6 -> x10, waiting for transfers between devices: 26.8 us -> 22.3 us  [the longest x9 21.3 us: send(): return lax.ppermute(value, 'seq', pairs)]
    psum x1 -> x0, blocking collectives: 4.22 us -> none  [on_device(): total = lax.psum(partial_value, 'tp')]
    ppermute x2 -> x0, local copies, waits for them, and re-layouts: 2.49 us -> none  [shifted(): lax.ppermute(value, axis, [(source, source + steps) for source in range(i...]
    reshape x1 -> x0, local copies, waits for them, and re-layouts: 2.04 us -> none  [absorb(): value_block.reshape(tok_rows, head_count, HEAD_DIM)]
  transfers between devices with their start and end apart: 6 -> 10, of which waited for: 4 -> 5; matrix products, arithmetic and copies ran while one was open for 20% -> 1% of each run, Pallas kernels for 0% -> 17%
where the time goes in v1:
time: 54.9 us; the launch traced here: 54.3 us
  waiting for transfers between devices  22.3 us (41%)
  Pallas kernels  14.8 us (27%)
  starting transfers between devices  9.45 us (17%)
  local copies, waits for them, and re-layouts  7.27 us (13%)
    ppermute x9, waiting for transfers between devices, send(): return lax.ppermute(value, 'seq', pairs)  21.3 us
    pallas_call x4, Pallas kernels, attend(): pl.pallas_call(functools.partial(attend_kernel, last), grid=(1,), out_sha...  12.6 us
    ppermute x9, starting transfers between devices, send(): return lax.ppermute(value, 'seq', pairs)  7.07 us
    unnamed x20, local copies, waits for them, and re-layouts  5.9 us
    ppermute x1, starting transfers between devices, on_device(): other = lax.ppermute(q, 'tp', [(i, i ^ 1) for i in range(tp)])  2.38 us
    pallas_call x1, Pallas kernels, on_device(): pl.pallas_call(functools.partial(finish_kernel, float(feat * tp)), out_sh...  2.23 us
    slice x1, local copies, waits for them, and re-layouts, on_device(): chunk.append(jnp.concatenate([keys[:, cols], values[:, cols]], axis=1))  1.36 us
  transfers between devices with their start and end apart: 10, of which 5 were waited for; matrix products, arithmetic and copies ran while one was open for 1% of the time, Pallas kernels for 17%

profile of v1, /device:TPU:11, one launch (start us, length us, event | category | flops | bytes accessed | tf_op | source)
XLA Modules:
  0.0 54.3 jit_solution(9077236350822052199)
XLA Ops:
  0.0 1.4 %fusion.2 = (bf16[256,256]{1,0:T(8,128)(2,1)S(1)}, bf16[256,256]{1,0:T(8,128)(2,1)S(1)}, bf16[256,256]{1,0:T(8,128)(2,1)S(1)}, bf16[256,256]{1,0:T(8,128)(2,1)S(...) fusion(bf16[256,1024]{1,0:T(8,128)(2,1)} %refs_1_.7, ...), kind=kLoop, calls=%fused_computation.10 | loop fusion | bytes 2097152 | tf_op jit(solution)/shard_map/slice | solution.py:122
  1.4 1.3 %collective-permute-start.7 = (bf16[256,512]{1,0:T(8,128)(2,1)S(1)}, bf16[256,512]{1,0:T(8,128)(2,1)S(1)}, u32[]{:S(2)}, u32[]{:S(2)}) collective-permute-start(bf16[256,512]{1,0:T(8,128)(2,1)S(1)} %pad_maximum_fusion.2), channel_id=1, source_target_pairs={{0,4},{2,6},{4,8},{6,10},{8,12},{10,14},{12,0},{14,2},{1,5},{3,7},... | collective-permute-start | bytes 786440 | tf_op jit(solution)/shard_map/ppermute | solution.py:115
  2.8 0.3 collective-permute-start.2
  3.1 3.2 %collective-permute-start.4 = (bf16[256,512]{1,0:T(8,128)(2,1)S(1)}, bf16[256,512]{1,0:T(8,128)(2,1)S(1)}, u32[]{:S(2)}, u32[]{:S(2)}) collective-permute-start(bf16[256,512]{1,0:T(8,128)(2,1)S(1)} %pad_maximum_fusion), channel_id=1, source_target_pairs={{0,4},{2,6},{4,8},{6,10},{8,12},{10,14},{1,5},{3,7},{5,9},{7,11},{... | collective-permute-start | bytes 786440 | tf_op jit(solution)/shard_map/ppermute | solution.py:115
  6.3 0.0 copy-start.8
  6.3 0.1 collective-permute-start.5
  6.4 0.6 %copy-done.8 = s32[256]{0:T(256)S(1)} copy-done((s32[256]{0:T(256)S(1)}, s32[256]{0:T(256)}, u32[]{:S(2)}) %copy-start.8) | copy-done | bytes 1048
  7.0 0.1 collective-permute-start
  7.1 1.6 %collective-permute-done.7.refs_7_ = bf16[256,512]{1,0:T(8,128)(2,1)S(1)} collective-permute-done((bf16[256,512]{1,0:T(8,128)(2,1)S(1)}, bf16[256,512]{1,0:T(8,128)(2,1)S(1)}, u32[]{:S(2)}, u32[]{:S(2)}) %collective-permute-start.7) | collective-permute-done | bytes 262176 | tf_op jit(solution)/shard_map/ppermute | solution.py:115
  8.6 0.0 copy-start.3
  8.6 0.1 broadcast_select_fusion.1
  8.7 0.6 %copy-done.3 = bf16[256,512]{1,0:T(8,128)(2,1)} copy-done((bf16[256,512]{1,0:T(8,128)(2,1)}, bf16[256,512]{1,0:T(8,128)(2,1)S(1)}, u32[]{:S(2)}) %copy-start.3) | copy-done | bytes 262168
  9.3 0.3 collective-permute-start.8
  9.6 10.3 %collective-permute-done.5.refs_7_ = bf16[256,512]{1,0:T(8,128)(2,1)S(1)} collective-permute-done((bf16[256,512]{1,0:T(8,128)(2,1)S(1)}, bf16[256,512]{1,0:T(8,128)(2,1)S(1)}, u32[]{:S(2)}, u32[]{:S(2)}) %collective-permute-start.5) | collective-permute-done | bytes 262176 | tf_op jit(solution)/shard_map/ppermute | solution.py:115
  19.9 0.0 copy-start.4
  19.9 0.1 broadcast_select_fusion.2
  19.9 0.6 %copy-done.4 = bf16[256,512]{1,0:T(8,128)(2,1)} copy-done((bf16[256,512]{1,0:T(8,128)(2,1)}, bf16[256,512]{1,0:T(8,128)(2,1)S(1)}, u32[]{:S(2)}) %copy-start.4) | copy-done | bytes 262168
  20.6 0.3 collective-permute-start.6
  20.8 5.0 %collective-permute-done.refs_5_.refs_7_ = bf16[272,512]{1,0:T(8,128)(2,1)S(1)} collective-permute-done((bf16[272,512]{1,0:T(8,128)(2,1)S(1)}, bf16[272,512]{1,0:T(8,128)(2,1)S(1)}, u32[]{:S(2)}, u32[]{:S(2)}) %collective-permute-start) | collective-permute-done | bytes 278560 | tf_op jit(solution)/shard_map/ppermute | solution.py:115
  25.8 0.0 copy-start
  25.8 0.1 broadcast_select_fusion
  25.9 0.6 %copy-done = bf16[272,512]{1,0:T(8,128)(2,1)} copy-done((bf16[272,512]{1,0:T(8,128)(2,1)}, bf16[272,512]{1,0:T(8,128)(2,1)S(1)}, u32[]{:S(2)}) %copy-start) | copy-done | bytes 278552
  26.6 0.3 collective-permute-start.1
  26.8 0.0 collective-permute-done.2.refs_6_
  26.8 0.0 copy-start.2
  26.8 0.1 broadcast_select_fusion.3
  26.9 0.6 %copy-done.2 = bf16[256,512]{1,0:T(8,128)(2,1)} copy-done((bf16[256,512]{1,0:T(8,128)(2,1)}, bf16[256,512]{1,0:T(8,128)(2,1)S(1)}, u32[]{:S(2)}) %copy-start.2) | copy-done | bytes 262168
  27.5 1.3 %collective-permute-start.3 = (bf16[256,512]{1,0:T(8,128)(2,1)S(1)}, bf16[256,512]{1,0:T(8,128)(2,1)S(1)}, u32[]{:S(2)}, u32[]{:S(2)}) collective-permute-start(bf16[256,512]{1,0:T(8,128)(2,1)S(1)} %broadcast_select_fusion.3), channel_id=1, source_target_pairs={{0,4},{2,6},{4,8},{6,10},{8,12},{10,14},{12,0},{14,2},{1,5},{3,7},... | collective-permute-start | bytes 786440 | tf_op jit(solution)/shard_map/ppermute | solution.py:115
  28.8 4.4 %collective-permute-done.1.refs_4_.refs_6_ = bf16[272,512]{1,0:T(8,128)(2,1)S(1)} collective-permute-done((bf16[272,512]{1,0:T(8,128)(2,1)S(1)}, bf16[272,512]{1,0:T(8,128)(2,1)S(1)}, u32[]{:S(2)}, u32[]{:S(2)}) %collective-permute-start.1) | collective-permute-done | bytes 278560 | tf_op jit(solution)/shard_map/ppermute | solution.py:115
  33.2 0.0 copy-start.1
  33.2 0.7 %copy-done.1 = bf16[272,512]{1,0:T(8,128)(2,1)} copy-done((bf16[272,512]{1,0:T(8,128)(2,1)}, bf16[272,512]{1,0:T(8,128)(2,1)S(1)}, u32[]{:S(2)}) %copy-start.1) | copy-done | bytes 278552
  34.0 3.1 %attend.3 = (bf16[256,256]{1,0:T(8,128)(2,1)}, f32[256,128]{1,0:T(8,128)}) custom-call(s32[1]{0:T(128)} %bitcast.me_ref, bf16[256,1024]{1,0:T(8,128)(2,1)} %refs_0_.7, bf16[256,1024]{1,0:T(8,128)(2,1)} %refs_1_.7, bf16[256,1024]{1,0:T(8,128)(2,1)} %refs_2_.7, s32[1,256]{1,0:T(1,128)} %bitcast.3, bf16[272,512]{1,0:T(8,128)(2,1)} %copy-done.1, ...), custom_call_target="tpu_custom_call" | custom-call | flops 201326592 | bytes 1310720 | tf_op jit(solution)/shard_map/attend/pallas_call | solution.py:145
  37.1 0.0 collective-permute-done.8.refs_6_
  37.1 3.1 %attend.5 = (bf16[256,256]{1,0:T(8,128)(2,1)}, f32[256,128]{1,0:T(8,128)}) custom-call(s32[1]{0:T(128)} %bitcast.me_ref, bf16[256,1024]{1,0:T(8,128)(2,1)} %refs_0_.7, bf16[256,1024]{1,0:T(8,128)(2,1)} %refs_1_.7, bf16[256,1024]{1,0:T(8,128)(2,1)} %refs_2_.7, s32[1,256]{1,0:T(1,128)} %bitcast.4, bf16[272,512]{1,0:T(8,128)(2,1)} %copy-done.1, ...), custom_call_target="tpu_custom_call" | custom-call | flops 201326592 | bytes 1310720 | tf_op jit(solution)/shard_map/attend/pallas_call | solution.py:145
  40.2 0.0 collective-permute-done.6.refs_6_
  40.2 0.0 copy-start.6
  40.2 0.7 %copy-done.6 = bf16[256,512]{1,0:T(8,128)(2,1)} copy-done((bf16[256,512]{1,0:T(8,128)(2,1)}, bf16[256,512]{1,0:T(8,128)(2,1)S(1)}, u32[]{:S(2)}) %copy-start.6) | copy-done | bytes 262168
  40.9 3.1 %attend.4 = (bf16[256,256]{1,0:T(8,128)(2,1)}, f32[256,128]{1,0:T(8,128)}) custom-call(s32[1]{0:T(128)} %bitcast.me_ref, bf16[256,1024]{1,0:T(8,128)(2,1)} %refs_0_.7, bf16[256,1024]{1,0:T(8,128)(2,1)} %refs_1_.7, bf16[256,1024]{1,0:T(8,128)(2,1)} %refs_2_.7, s32[1,256]{1,0:T(1,128)} %bitcast.5, bf16[272,512]{1,0:T(8,128)(2,1)} %copy-done.1, ...), custom_call_target="tpu_custom_call" | custom-call | flops 201326592 | bytes 1310720 | tf_op jit(solution)/shard_map/attend/pallas_call | solution.py:145
  44.0 0.0 collective-permute-done.4.refs_8_
  44.0 0.0 copy-start.5
  44.0 0.0 collective-permute-done.3.refs_7_
  44.0 0.0 copy-start.7
  44.1 0.7 %copy-done.5 = bf16[256,512]{1,0:T(8,128)(2,1)} copy-done((bf16[256,512]{1,0:T(8,128)(2,1)}, bf16[256,512]{1,0:T(8,128)(2,1)S(1)}, u32[]{:S(2)}) %copy-start.5) | copy-done | bytes 262168
  44.7 0.1 copy-done.7
  44.8 3.3 %attend_last.1 = (bf16[256,256]{1,0:T(8,128)(2,1)}, f32[8,256]{1,0:T(8,128)}) custom-call(s32[1]{0:T(128)} %bitcast.me_ref, bf16[256,1024]{1,0:T(8,128)(2,1)} %refs_0_.7, bf16[256,1024]{1,0:T(8,128)(2,1)} %refs_1_.7, bf16[256,1024]{1,0:T(8,128)(2,1)} %refs_2_.7, s32[1,256]{1,0:T(1,128)} %bitcast.6, bf16[272,512]{1,0:T(8,128)(2,1)} %copy-done.1, ...), custom_call_target="tpu_custom_call" | custom-call | flops 201326592 | bytes 1310720 | tf_op jit(solution)/shard_map/attend_last/pallas_call | solution.py:145
  48.1 2.4 %collective-permute-start.9 = (f32[8,256]{1,0:T(8,128)}, f32[8,256]{1,0:T(8,128)S(1)}, u32[]{:S(2)}, u32[]{:S(2)}) collective-permute-start(f32[8,256]{1,0:T(8,128)} %get-tuple-element.16.mine_ref), channel_id=1, source_target_pairs={{0,1},{1,0},{2,3},{3,2},{4,5},{5,4},{6,7},{7,6},{8,9},{9,8},{10,11... | collective-permute-start | bytes 24584 | tf_op jit(solution)/shard_map/ppermute | solution.py:163
  50.5 1.0 %collective-permute-done.9.other_ref = f32[8,256]{1,0:T(8,128)S(1)} collective-permute-done((f32[8,256]{1,0:T(8,128)}, f32[8,256]{1,0:T(8,128)S(1)}, u32[]{:S(2)}, u32[]{:S(2)}) %collective-permute-start.9) | collective-permute-done | bytes 8224 | tf_op jit(solution)/shard_map/ppermute | solution.py:163
  51.5 0.0 copy-start.9
  51.5 0.6 %copy-done.9 = f32[8,256]{1,0:T(8,128)} copy-done((f32[8,256]{1,0:T(8,128)}, f32[8,256]{1,0:T(8,128)S(1)}, u32[]{:S(2)}) %copy-start.9) | copy-done | bytes 8216
  52.1 2.2 %finish.1 = bf16[256,1024]{1,0:T(8,128)(2,1)} custom-call(f32[8,256]{1,0:T(8,128)} %get-tuple-element.16.mine_ref, f32[8,256]{1,0:T(8,128)} %copy-done.9, s32[1,256]{1,0:T(1,128)} %bitcast.7, f32[2,1024]{1,0:T(2,128)} %gain_ref.1, bf16[256,256]{1,0:T(8,128)(2,1)} %get-tuple-element.17.refs_0_, bf16[256,256]{1,0:T(8,128)(2,1)} %get-tuple-element.18.refs_1_, ...), custom_call_target="tpu_custom_call" | custom-call | tf_op jit(solution)/shard_map/finish/pallas_call | solution.py:164
  (6 shorter events, 0.1 us)
Async XLA Ops:
  1.4 7.2 %collective-permute-start.7 = (bf16[256,512]{1,0:T(8,128)(2,1)S(1)}, bf16[256,512]{1,0:T(8,128)(2,1)S(1)}, u32[]{:S(2)}, u32[]{:S(2)}) collective-permute-start(bf16[256,512]{1,0:T(8,128)(2,1)S(1)} %pad_maximum_fusion.2), channel_id=1, source_target_pairs={{0,4},{2,6},{4,8},{6,10},{8,12},{10,14},{12,0},{14,2},{1,5},{3,7},... | collective-permute-start | bytes 786440 | tf_op jit(solution)/shard_map/ppermute | solution.py:115
  2.8 24.0 %collective-permute-start.2 = (bf16[256,512]{1,0:T(8,128)(2,1)S(1)}, bf16[256,512]{1,0:T(8,128)(2,1)S(1)}, u32[]{:S(2)}, u32[]{:S(2)}) collective-permute-start(bf16[256,512]{1,0:T(8,128)(2,1)S(1)} %pad_maximum_fusion), channel_id=1, source_target_pairs={{0,2},{2,0},{4,6},{6,4},{8,10},{10,8},{12,14},{14,12},{1,3},{3,1},... | collective-permute-start | bytes 786440 | tf_op jit(solution)/shard_map/ppermute | solution.py:115
  3.1 40.9 %collective-permute-start.4 = (bf16[256,512]{1,0:T(8,128)(2,1)S(1)}, bf16[256,512]{1,0:T(8,128)(2,1)S(1)}, u32[]{:S(2)}, u32[]{:S(2)}) collective-permute-start(bf16[256,512]{1,0:T(8,128)(2,1)S(1)} %pad_maximum_fusion), channel_id=1, source_target_pairs={{0,4},{2,6},{4,8},{6,10},{8,12},{10,14},{1,5},{3,7},{5,9},{7,11},{... | collective-permute-start | bytes 786440 | tf_op jit(solution)/shard_map/ppermute | solution.py:115
  6.3 0.7 %copy-start.8 = (s32[256]{0:T(256)S(1)}, s32[256]{0:T(256)}, u32[]{:S(2)}) copy-start(s32[256]{0:T(256)} %param.9) | copy-start | bytes 3076
  6.3 13.5 %collective-permute-start.5 = (bf16[256,512]{1,0:T(8,128)(2,1)S(1)}, bf16[256,512]{1,0:T(8,128)(2,1)S(1)}, u32[]{:S(2)}, u32[]{:S(2)}) collective-permute-start(bf16[256,512]{1,0:T(8,128)(2,1)S(1)} %pad_maximum_fusion.1), channel_id=1, source_target_pairs={{0,4},{2,6},{4,8},{6,10},{8,12},{10,14},{12,0},{14,2},{1,5},{3,7},... | collective-permute-start | bytes 786440 | tf_op jit(solution)/shard_map/ppermute | solution.py:115
  7.0 18.8 %collective-permute-start = (bf16[272,512]{1,0:T(8,128)(2,1)S(1)}, bf16[272,512]{1,0:T(8,128)(2,1)S(1)}, u32[]{:S(2)}, u32[]{:S(2)}) collective-permute-start(bf16[272,512]{1,0:T(8,128)(2,1)S(1)} %fusion.1), channel_id=1, source_target_pairs={{0,4},{2,6},{4,8},{6,10},{8,12},{10,14},{12,0},{14,2},{1,5},{3,7},... | collective-permute-start | bytes 835592 | tf_op jit(solution)/shard_map/ppermute | solution.py:115
  8.6 0.7 %copy-start.3 = (bf16[256,512]{1,0:T(8,128)(2,1)}, bf16[256,512]{1,0:T(8,128)(2,1)S(1)}, u32[]{:S(2)}) copy-start(bf16[256,512]{1,0:T(8,128)(2,1)S(1)} %collective-permute-done.7.refs_7_) | copy-start | bytes 786436
  9.3 27.7 %collective-permute-start.8 = (bf16[256,512]{1,0:T(8,128)(2,1)S(1)}, bf16[256,512]{1,0:T(8,128)(2,1)}, u32[]{:S(2)}, u32[]{:S(2)}) collective-permute-start(bf16[256,512]{1,0:T(8,128)(2,1)S(1)} %broadcast_select_fusion.1), channel_id=1, source_target_pairs={{0,2},{2,0},{4,6},{6,4},{8,10},{10,8},{12,14},{14,12},{1,3},{3,1},... | collective-permute-start | bytes 786440 | tf_op jit(solution)/shard_map/ppermute | solution.py:115
  19.9 0.7 %copy-start.4 = (bf16[256,512]{1,0:T(8,128)(2,1)}, bf16[256,512]{1,0:T(8,128)(2,1)S(1)}, u32[]{:S(2)}) copy-start(bf16[256,512]{1,0:T(8,128)(2,1)S(1)} %collective-permute-done.5.refs_7_) | copy-start | bytes 786436
  20.6 19.6 %collective-permute-start.6 = (bf16[256,512]{1,0:T(8,128)(2,1)S(1)}, bf16[256,512]{1,0:T(8,128)(2,1)S(1)}, u32[]{:S(2)}, u32[]{:S(2)}) collective-permute-start(bf16[256,512]{1,0:T(8,128)(2,1)S(1)} %broadcast_select_fusion.2), channel_id=1, source_target_pairs={{0,2},{2,0},{4,6},{6,4},{8,10},{10,8},{12,14},{14,12},{1,3},{3,1},... | collective-permute-start | bytes 786440 | tf_op jit(solution)/shard_map/ppermute | solution.py:115
  25.8 0.7 %copy-start = (bf16[272,512]{1,0:T(8,128)(2,1)}, bf16[272,512]{1,0:T(8,128)(2,1)S(1)}, u32[]{:S(2)}) copy-start(bf16[272,512]{1,0:T(8,128)(2,1)S(1)} %collective-permute-done.refs_5_.refs_7_) | copy-start | bytes 835588
  26.6 6.7 %collective-permute-start.1 = (bf16[272,512]{1,0:T(8,128)(2,1)S(1)}, bf16[272,512]{1,0:T(8,128)(2,1)S(1)}, u32[]{:S(2)}, u32[]{:S(2)}) collective-permute-start(bf16[272,512]{1,0:T(8,128)(2,1)S(1)} %broadcast_select_fusion), channel_id=1, source_target_pairs={{0,2},{2,0},{4,6},{6,4},{8,10},{10,8},{12,14},{14,12},{1,3},{3,1},... | collective-permute-start | bytes 835592 | tf_op jit(solution)/shard_map/ppermute | solution.py:115
  26.8 0.7 %copy-start.2 = (bf16[256,512]{1,0:T(8,128)(2,1)}, bf16[256,512]{1,0:T(8,128)(2,1)S(1)}, u32[]{:S(2)}) copy-start(bf16[256,512]{1,0:T(8,128)(2,1)S(1)} %collective-permute-done.2.refs_6_) | copy-start | bytes 786436
  27.5 16.5 %collective-permute-start.3 = (bf16[256,512]{1,0:T(8,128)(2,1)S(1)}, bf16[256,512]{1,0:T(8,128)(2,1)S(1)}, u32[]{:S(2)}, u32[]{:S(2)}) collective-permute-start(bf16[256,512]{1,0:T(8,128)(2,1)S(1)} %broadcast_select_fusion.3), channel_id=1, source_target_pairs={{0,4},{2,6},{4,8},{6,10},{8,12},{10,14},{12,0},{14,2},{1,5},{3,7},... | collective-permute-start | bytes 786440 | tf_op jit(solution)/shard_map/ppermute | solution.py:115
  33.2 0.7 %copy-start.1 = (bf16[272,512]{1,0:T(8,128)(2,1)}, bf16[272,512]{1,0:T(8,128)(2,1)S(1)}, u32[]{:S(2)}) copy-start(bf16[272,512]{1,0:T(8,128)(2,1)S(1)} %collective-permute-done.1.refs_4_.refs_6_) | copy-start | bytes 835588
  40.2 0.7 %copy-start.6 = (bf16[256,512]{1,0:T(8,128)(2,1)}, bf16[256,512]{1,0:T(8,128)(2,1)S(1)}, u32[]{:S(2)}) copy-start(bf16[256,512]{1,0:T(8,128)(2,1)S(1)} %collective-permute-done.6.refs_6_) | copy-start | bytes 786436
  44.0 0.7 %copy-start.5 = (bf16[256,512]{1,0:T(8,128)(2,1)}, bf16[256,512]{1,0:T(8,128)(2,1)S(1)}, u32[]{:S(2)}) copy-start(bf16[256,512]{1,0:T(8,128)(2,1)S(1)} %collective-permute-done.4.refs_8_) | copy-start | bytes 786436
  44.0 0.8 %copy-start.7 = (bf16[256,512]{1,0:T(8,128)(2,1)}, bf16[256,512]{1,0:T(8,128)(2,1)S(1)}, u32[]{:S(2)}) copy-start(bf16[256,512]{1,0:T(8,128)(2,1)S(1)} %collective-permute-done.3.refs_7_) | copy-start | bytes 786436
  48.1 3.4 %collective-permute-start.9 = (f32[8,256]{1,0:T(8,128)}, f32[8,256]{1,0:T(8,128)S(1)}, u32[]{:S(2)}, u32[]{:S(2)}) collective-permute-start(f32[8,256]{1,0:T(8,128)} %get-tuple-element.16.mine_ref), channel_id=1, source_target_pairs={{0,1},{1,0},{2,3},{3,2},{4,5},{5,4},{6,7},{7,6},{8,9},{9,8},{10,11... | collective-permute-start | bytes 24584 | tf_op jit(solution)/shard_map/ppermute | solution.py:163
  51.5 0.6 %copy-start.9 = (f32[8,256]{1,0:T(8,128)}, f32[8,256]{1,0:T(8,128)S(1)}, u32[]{:S(2)}) copy-start(f32[8,256]{1,0:T(8,128)S(1)} %collective-permute-done.9.other_ref) | copy-start | bytes 24580

commit v2 on v1

--- a/solution.py
+++ b/solution.py
@@ -14,6 +14,7 @@
 SEG_ROWS = 16
 NEG = -1e30
 EPS = 1e-05
+VMEM_LIMIT = 12 * 1024 * 1024
 
 
 def column(row):
@@ -52,30 +53,72 @@
     return (acc / total).astype(jnp.bfloat16)
 
 
-def attend_kernel(last, me_ref, *refs):
-    q_ref, k_ref, v_ref, seg_ref, near_seg_ref, far_seg_ref = refs[:6]
+def pack_kernel(me_ref, keys_ref, values_ref, seg_ref, mod_ref, chunk_ref, aux_ref, ids_ref, sem):
+    tok, width = keys_ref.shape[0], keys_ref.shape[1] // CHUNKS
+    copies = [
+        pltpu.make_async_copy(seg_ref, ids_ref.at[0], sem.at[0]),
+        pltpu.make_async_copy(mod_ref, ids_ref.at[1], sem.at[1]),
+        pltpu.make_async_copy(keys_ref.at[:, 0:width], chunk_ref.at[0:tok, 0:width], sem.at[2]),
+        pltpu.make_async_copy(values_ref.at[:, 0:width], chunk_ref.at[0:tok, width : 2 * width], sem.at[3]),
+    ]
+    for copy in copies:
+        copy.start()
+    copies[0].wait()
+    copies[1].wait()
+    seg = ids_ref[0].astype(jnp.float32)
+    mod = ids_ref[1].astype(jnp.float32)
+    aux_ref[0:1, :] = seg
+    aux_ref[1:2, :] = mod
+    aux_ref[2:8, :] = jnp.zeros((6, tok), jnp.float32)
+    chunk_ref[tok : tok + SEG_ROWS, 0:tok] = jnp.broadcast_to(seg, (SEG_ROWS, tok)).astype(jnp.bfloat16)
+    chunk_ref[tok : tok + SEG_ROWS, tok:] = jnp.zeros((SEG_ROWS, 2 * width - tok), jnp.bfloat16)
+    copies[2].wait()
+    copies[3].wait()
+
+
+def pack_rest_kernel(keys_ref, values_ref, *refs):
+    chunk_refs, sem = refs[:-1], refs[-1]
+    width = keys_ref.shape[1] // CHUNKS
+    copies = []
+    for c, chunk_ref in enumerate(chunk_refs, 1):
+        cols = slice(c * width, (c + 1) * width)
+        copies.append(pltpu.make_async_copy(keys_ref.at[:, cols], chunk_ref.at[:, 0:width], sem.at[2 * c - 2]))
+        copies.append(
+            pltpu.make_async_copy(values_ref.at[:, cols], chunk_ref.at[:, width : 2 * width], sem.at[2 * c - 1])
+        )
+    for copy in copies:
+        copy.start()
+    for copy in copies:
+        copy.wait()
+
+
+def attend_kernel(c, last, me_ref, *refs):
+    q_ref, own_ref, aux_ref, near_seg_ref, far_seg_ref = refs[:5]
     me = me_ref[0]
-    tok, width = q_ref.shape
-    seg = seg_ref[...].astype(jnp.float32)
-    near_seg = near_seg_ref[...][0:1, :tok].astype(jnp.float32)
-    far_seg = far_seg_ref[...][0:1, :tok].astype(jnp.float32)
-    masks = allowed_masks(me, seg, near_seg, far_seg)
+    tok, width = q_ref.shape[0], q_ref.shape[1] // CHUNKS
+    near_seg = near_seg_ref[tok : tok + SEG_ROWS, :tok][0:1, :].astype(jnp.float32)
+    far_seg = far_seg_ref[tok : tok + SEG_ROWS, :tok][0:1, :].astype(jnp.float32)
+    masks = allowed_masks(me, aux_ref[0:1, :], near_seg, far_seg)
     if last:
-        s_ref, f_ref, a_ref, p0, p1, p2 = refs[6:12]
-        att_ref, sq_ref = refs[12:]
+        s_ref, f_ref, a_ref, p0, p1, p2 = refs[5:11]
+        att_ref, sq_ref = refs[11:]
         odd = lax.rem(me, 2) == 1
         near = jnp.where(odd, s_ref[...], f_ref[...])
         far = jnp.where(odd, f_ref[...], a_ref[...])
     else:
-        near_ref, far_ref = refs[6:8]
-        att_ref, sq_ref = refs[8:]
+        near_ref, far_ref = refs[5:7]
+        att_ref, sq_ref = refs[7:]
         near, far = near_ref[:tok, :], far_ref[:tok, :]
     squares = None
     for h in range(width // HEAD_DIM):
         ks = slice(h * HEAD_DIM, (h + 1) * HEAD_DIM)
         vs = slice(width + h * HEAD_DIM, width + (h + 1) * HEAD_DIM)
+        own = slice(c * width + h * HEAD_DIM, c * width + (h + 1) * HEAD_DIM)
         att = attend_head(
-            q_ref[:, ks], (k_ref[:, ks], near[:, ks], far[:, ks]), (v_ref[:, ks], near[:, vs], far[:, vs]), masks
+            q_ref[:, own],
+            (own_ref[:tok, ks], near[:, ks], far[:, ks]),
+            (own_ref[:tok, vs], near[:, vs], far[:, vs]),
+            masks,
         )
         att_ref[:, ks] = att
         att = att.astype(jnp.float32)
@@ -87,11 +130,11 @@
         sq_ref[...] = squares
 
 
-def finish_kernel(features, mine_ref, other_ref, mod_ref, gain_ref, *refs):
+def finish_kernel(features, mine_ref, other_ref, aux_ref, gain_ref, *refs):
     att_refs, out_ref = refs[:-1], refs[-1]
     total = jnp.sum(mine_ref[...] + other_ref[...], axis=0, keepdims=True)
     inverse = column(lax.rsqrt(total / features + EPS))
-    image = column(mod_ref[...].astype(jnp.float32)) == 1.0
+    image = column(aux_ref[1:2, :]) == 1.0
     for c, att_ref in enumerate(att_refs):
         width = att_ref.shape[1]
         for b in range(width // 128):
@@ -114,43 +157,59 @@
     def send(value, pairs):
         return lax.ppermute(value, "seq", pairs)
 
-    seg_row = segment_ids.astype(jnp.bfloat16)
-    seg_block = jnp.pad(seg_row[None, :], ((0, SEG_ROWS - 1), (0, 2 * width - tok)))
-    chunk = []
-    for c in range(CHUNKS):
-        cols = slice(c * width, (c + 1) * width)
-        chunk.append(jnp.concatenate([keys[:, cols], values[:, cols]], axis=1))
-    chunk[0] = jnp.concatenate([chunk[0], seg_block], axis=0)
+    def pick(at_odd, at_even):
+        return jnp.where(odd, at_odd, at_even)
+
+    smem = pl.BlockSpec(memory_space=pltpu.SMEM)
+    vmem = pl.BlockSpec(memory_space=pltpu.VMEM)
+    hbm = pl.BlockSpec(memory_space=pltpu.HBM)
+    small = pltpu.CompilerParams(vmem_limit_bytes=VMEM_LIMIT)
+    me1 = me.astype(jnp.int32)[None]
+    first, aux = pl.pallas_call(
+        pack_kernel,
+        out_shape=(
+            jax.ShapeDtypeStruct((tok + SEG_ROWS, 2 * width), jnp.bfloat16),
+            jax.ShapeDtypeStruct((8, tok), jnp.float32),
+        ),
+        in_specs=[smem, hbm, hbm, hbm, hbm],
+        out_specs=(vmem, vmem),
+        scratch_shapes=[pltpu.VMEM((2, 1, tok), jnp.int32), pltpu.SemaphoreType.DMA((4,))],
+        name="pack",
+        compiler_params=small,
+    )(me1, keys, values, segment_ids[None, :], modality[None, :])
+    rest = pl.pallas_call(
+        pack_rest_kernel,
+        out_shape=tuple(jax.ShapeDtypeStruct((tok, 2 * width), jnp.bfloat16) for _ in range(CHUNKS - 1)),
+        in_specs=[hbm, hbm],
+        out_specs=(vmem,) * (CHUNKS - 1),
+        scratch_shapes=[pltpu.SemaphoreType.DMA((2 * CHUNKS - 2,))],
+        name="pack_rest",
+        compiler_params=small,
+    )(keys, values)
+    chunk = (first, *rest)
     a0 = send(chunk[0], ring2)
     s = send(chunk[3], pair)
     a1 = send(chunk[1], ring2)
     a2 = send(chunk[2], ring2)
-    x0 = send(jnp.where(odd, a0, chunk[0]), pair)
-    f = send(jnp.where(odd, chunk[3], s), ring2)
-    x1 = send(jnp.where(odd, a1, chunk[1]), pair)
+    x0 = send(pick(a0, chunk[0]), pair)
+    f = send(pick(chunk[3], s), ring2)
+    x1 = send(pick(a1, chunk[1]), pair)
     a3 = send(chunk[3], shift2)
-    x2 = send(jnp.where(odd, a2, chunk[2]), pair)
-
-    seg2d = segment_ids[None, :]
-    me1 = me.astype(jnp.int32)[None]
-    smem = pl.BlockSpec(memory_space=pltpu.SMEM)
-    whole = lambda a: pl.BlockSpec(a.shape, lambda i: (0,) * len(a.shape))
-    segs = pl.BlockSpec((SEG_ROWS, 2 * width), lambda i: (tok // SEG_ROWS, 0))
+    x2 = send(pick(a2, chunk[2]), pair)
+
     flops = 3 * 4 * tok * tok * width
 
     def attend(c, last, rest):
-        cols = pl.BlockSpec((tok, width), lambda i: (0, c))
         sq_shape = (8, tok) if last else (tok, 128)
         outs = (jax.ShapeDtypeStruct((tok, width), jnp.bfloat16), jax.ShapeDtypeStruct(sq_shape, jnp.float32))
         return pl.pallas_call(
-            functools.partial(attend_kernel, last),
-            grid=(1,),
+            functools.partial(attend_kernel, c, last),
             out_shape=outs,
-            out_specs=tuple(whole(o) for o in outs),
-            in_specs=[smem, cols, cols, cols, whole(seg2d), segs, segs] + [whole(r) for r in rest],
-            name="attend_last" if last else "attend",
+            out_specs=(vmem, vmem),
+            in_specs=[smem] + [vmem] * (5 + len(rest)),
+            compiler_params=small,
             cost_estimate=pl.CostEstimate(flops=flops, bytes_accessed=tok * width * 20, transcendentals=3 * tok * tok * 2),
-        )(me1, queries, keys, values, seg2d, x0, a0, *rest)
+        )(me1, queries, chunk[c], aux, x0, a0, *rest)
 
     att, sq = [], []
     for c, (near, far) in enumerate(((x0, a0), (x1, a1), (x2, a2))):
@@ -164,8 +223,11 @@
     return pl.pallas_call(
         functools.partial(finish_kernel, float(feat * tp)),
         out_shape=jax.ShapeDtypeStruct((tok, feat), jnp.bfloat16),
+        in_specs=[vmem] * (4 + CHUNKS),
+        out_specs=vmem,
         name="finish",
-    )(q, other, modality[None, :], norm_gain, *att)
+        compiler_params=small,
+    )(q, other, aux, norm_gain, *att)
 
 
 def solution(mesh):

time: 54.9 us -> 43.3 us (0.79)
  Pallas kernels: 14.8 us -> 5.98 us
  local copies, waits for them, and re-layouts: 7.27 us -> 2.76 us
  starting transfers between devices: 9.45 us -> 11.5 us
    pallas_call x4 -> x6, Pallas kernels: 12.6 us -> 4.91 us  [the longest x4 4.65 us: attend(): pl.pallas_call(functools.partial(attend_kernel, c, last), out_shape=outs,...]
    unnamed x20 -> x16, local copies, waits for them, and re-layouts: 5.9 us -> 2.76 us
    ppermute x9, starting transfers between devices: 7.07 us -> 9 us  [send(): return lax.ppermute(value, 'seq', pairs)]
    slice x1 -> x0, local copies, waits for them, and re-layouts: 1.36 us -> none  [on_device(): chunk.append(jnp.concatenate([keys[:, cols], values[:, cols]], axis=1))]
    pallas_call x1, Pallas kernels: 2.23 us -> 1.07 us  [on_device(): pl.pallas_call(functools.partial(finish_kernel, float(feat * tp)), out_sh...]
  transfers between devices with their start and end apart: 10 -> 10, of which waited for: 5 -> 5; matrix products, arithmetic and copies ran while one was open for 1% -> 0% of each run, Pallas kernels for 17% -> 8%
where the time goes in v2:
time: 43.3 us; the launch traced here: 42.6 us
  waiting for transfers between devices  22.1 us (51%)
  starting transfers between devices  11.5 us (27%)
  Pallas kernels  5.98 us (14%)
  local copies, waits for them, and re-layouts  2.76 us (6%)
    ppermute x9, waiting for transfers between devices, send(): return lax.ppermute(value, 'seq', pairs)  21.3 us
    ppermute x9, starting transfers between devices, send(): return lax.ppermute(value, 'seq', pairs)  9 us
    pallas_call x4, Pallas kernels, attend(): pl.pallas_call(functools.partial(attend_kernel, c, last), out_shape=outs,...  4.65 us
    unnamed x16, local copies, waits for them, and re-layouts  2.76 us
    ppermute x1, starting transfers between devices, on_device(): other = lax.ppermute(q, 'tp', [(i, i ^ 1) for i in range(tp)])  2.45 us
    pallas_call x1, Pallas kernels, on_device(): pl.pallas_call(functools.partial(finish_kernel, float(feat * tp)), out_sh...  1.07 us
  transfers between devices with their start and end apart: 10, of which 5 were waited for; matrix products, arithmetic and copies ran while one was open for 0% of the time, Pallas kernels for 8%

profile of v2, /device:TPU:11, one launch (start us, length us, event | category | flops | bytes accessed | tf_op | source)
XLA Modules:
  0.0 42.6 jit_solution(7683095646631343959)
XLA Ops:
  0.0 0.0 copy-start.1
  0.0 1.0 %copy-done.1 = bf16[256,1024]{1,0:T(8,128)(2,1)S(1)} copy-done((bf16[256,1024]{1,0:T(8,128)(2,1)S(1)}, bf16[256,1024]{1,0:T(8,128)(2,1)}, u32[]{:S(2)}) %copy-start.1) | copy-done | bytes 524312
  1.0 0.0 copy-start.3
  1.0 1.0 %copy-done.3 = bf16[256,1024]{1,0:T(8,128)(2,1)S(1)} copy-done((bf16[256,1024]{1,0:T(8,128)(2,1)S(1)}, bf16[256,1024]{1,0:T(8,128)(2,1)}, u32[]{:S(2)}) %copy-start.3) | copy-done | bytes 524312
  2.1 0.0 copy-start.2
  2.1 0.0 copy-start.4
  2.1 0.2 pack_rest.1
  2.3 1.3 %collective-permute-start.7 = (bf16[256,512]{1,0:T(8,128)(2,1)S(1)}, bf16[256,512]{1,0:T(8,128)(2,1)S(1)}, u32[]{:S(2)}, u32[]{:S(2)}) collective-permute-start(bf16[256,512]{1,0:T(8,128)(2,1)S(1)} %get-tuple-element.24.refs_1_), channel_id=1, source_target_pairs={{0,4},{2,6},{4,8},{6,10},{8,12},{10,14},{12,0},{14,2},{1,5},{3,7},... | collective-permute-start | bytes 786440 | tf_op jit(solution)/shard_map/ppermute | solution.py:158
  3.6 1.3 %collective-permute-start.5 = (bf16[256,512]{1,0:T(8,128)(2,1)S(1)}, bf16[256,512]{1,0:T(8,128)(2,1)S(1)}, u32[]{:S(2)}, u32[]{:S(2)}) collective-permute-start(bf16[256,512]{1,0:T(8,128)(2,1)S(1)} %get-tuple-element.22.refs_1_), channel_id=1, source_target_pairs={{0,4},{2,6},{4,8},{6,10},{8,12},{10,14},{12,0},{14,2},{1,5},{3,7},... | collective-permute-start | bytes 786440 | tf_op jit(solution)/shard_map/ppermute | solution.py:158
  4.9 0.3 collective-permute-start.2
  5.2 2.0 %collective-permute-start.4 = (bf16[256,512]{1,0:T(8,128)(2,1)S(1)}, bf16[256,512]{1,0:T(8,128)(2,1)S(1)}, u32[]{:S(2)}, u32[]{:S(2)}) collective-permute-start(bf16[256,512]{1,0:T(8,128)(2,1)S(1)} %get-tuple-element.18.refs_1_), channel_id=1, source_target_pairs={{0,4},{2,6},{4,8},{6,10},{8,12},{10,14},{1,5},{3,7},{5,9},{7,11},{... | collective-permute-start | bytes 786440 | tf_op jit(solution)/shard_map/ppermute | solution.py:158
  7.1 0.0 copy-start.7
  7.2 0.0 copy-start.6
  7.2 0.0 copy-done.2
  7.2 0.0 copy-done.4
  7.2 0.6 %copy-done.7 = s32[256]{0:T(256)S(1)} copy-done((s32[256]{0:T(256)S(1)}, s32[256]{0:T(256)}, u32[]{:S(2)}) %copy-start.7) | copy-done | bytes 1048
  7.8 0.0 copy-done.6
  7.8 0.1 pack.1
  7.9 1.2 %collective-permute-start = (bf16[272,512]{1,0:T(8,128)(2,1)S(1)}, bf16[272,512]{1,0:T(8,128)(2,1)S(1)}, u32[]{:S(2)}, u32[]{:S(2)}) collective-permute-start(bf16[272,512]{1,0:T(8,128)(2,1)S(1)} %get-tuple-element.20.refs_1_), channel_id=1, source_target_pairs={{0,4},{2,6},{4,8},{6,10},{8,12},{10,14},{12,0},{14,2},{1,5},{3,7},... | collective-permute-start | bytes 835592 | tf_op jit(solution)/shard_map/ppermute | solution.py:158
  9.2 0.4 collective-permute-done.7.refs_6_
  9.5 0.9 %collective-permute-start.8 = (bf16[256,512]{1,0:T(8,128)(2,1)S(1)}, bf16[256,512]{1,0:T(8,128)(2,1)S(1)}, u32[]{:S(2)}, u32[]{:S(2)}) collective-permute-start(bf16[256,512]{1,0:T(8,128)(2,1)S(1)} %broadcast_select_fusion.1), channel_id=1, source_target_pairs={{0,2},{2,0},{4,6},{6,4},{8,10},{10,8},{12,14},{14,12},{1,3},{3,1},... | collective-permute-start | bytes 786440 | tf_op jit(solution)/shard_map/ppermute | solution.py:158
  10.5 4.7 %collective-permute-done.5.refs_6_ = bf16[256,512]{1,0:T(8,128)(2,1)S(1)} collective-permute-done((bf16[256,512]{1,0:T(8,128)(2,1)S(1)}, bf16[256,512]{1,0:T(8,128)(2,1)S(1)}, u32[]{:S(2)}, u32[]{:S(2)}) %collective-permute-start.5) | collective-permute-done | bytes 262176 | tf_op jit(solution)/shard_map/ppermute | solution.py:158
  15.2 0.3 collective-permute-start.6
  15.5 11.2 %collective-permute-done.refs_4_.refs_6_ = bf16[272,512]{1,0:T(8,128)(2,1)S(1)} collective-permute-done((bf16[272,512]{1,0:T(8,128)(2,1)S(1)}, bf16[272,512]{1,0:T(8,128)(2,1)S(1)}, u32[]{:S(2)}, u32[]{:S(2)}) %collective-permute-start) | collective-permute-done | bytes 278560 | tf_op jit(solution)/shard_map/ppermute | solution.py:158
  26.7 0.0 copy-start
  26.8 0.3 collective-permute-start.1
  27.1 0.0 collective-permute-done.2.refs_5_
  27.1 1.3 %collective-permute-start.3 = (bf16[256,512]{1,0:T(8,128)(2,1)S(1)}, bf16[256,512]{1,0:T(8,128)(2,1)S(1)}, u32[]{:S(2)}, u32[]{:S(2)}) collective-permute-start(bf16[256,512]{1,0:T(8,128)(2,1)S(1)} %broadcast_select_fusion.3), channel_id=1, source_target_pairs={{0,4},{2,6},{4,8},{6,10},{8,12},{10,14},{12,0},{14,2},{1,5},{3,7},... | collective-permute-start | bytes 786440 | tf_op jit(solution)/shard_map/ppermute | solution.py:158
  28.5 5.0 %collective-permute-done.1.refs_3_.refs_5_ = bf16[272,512]{1,0:T(8,128)(2,1)S(1)} collective-permute-done((bf16[272,512]{1,0:T(8,128)(2,1)S(1)}, bf16[272,512]{1,0:T(8,128)(2,1)S(1)}, u32[]{:S(2)}, u32[]{:S(2)}) %collective-permute-start.1) | collective-permute-done | bytes 278560 | tf_op jit(solution)/shard_map/ppermute | solution.py:158
  33.5 0.0 copy-done
  33.5 1.1 %shard_map.64 = (bf16[256,256]{1,0:T(8,128)(2,1)S(1)}, f32[256,128]{1,0:T(8,128)S(1)}) custom-call(s32[1]{0:T(128)} %bitcast.me_ref, bf16[256,1024]{1,0:T(8,128)(2,1)S(1)} %copy-done, bf16[272,512]{1,0:T(8,128)(2,1)S(1)} %get-tuple-element.20.refs_1_, f32[8,256]{1,0:T(8,128)S(1)} %get-tuple-element.19.refs_2_.aux_ref, ...), custom_call_target="tpu_custom_call" | custom-call | flops 201326592 | bytes 1310720 | tf_op jit(solution)/shard_map/pallas_call | solution.py:205
  34.7 0.0 collective-permute-done.8.refs_5_
  34.7 1.1 %shard_map.66 = (bf16[256,256]{1,0:T(8,128)(2,1)S(1)}, f32[256,128]{1,0:T(8,128)S(1)}) custom-call(s32[1]{0:T(128)} %bitcast.me_ref, bf16[256,1024]{1,0:T(8,128)(2,1)S(1)} %copy-done, bf16[256,512]{1,0:T(8,128)(2,1)S(1)} %get-tuple-element.24.refs_1_, f32[8,256]{1,0:T(8,128)S(1)} %get-tuple-element.19.refs_2_.aux_ref, ...), custom_call_target="tpu_custom_call" | custom-call | flops 201326592 | bytes 1310720 | tf_op jit(solution)/shard_map/pallas_call | solution.py:205
  35.8 0.0 collective-permute-done.6.refs_5_
  35.8 1.1 %shard_map.65 = (bf16[256,256]{1,0:T(8,128)(2,1)S(1)}, f32[256,128]{1,0:T(8,128)S(1)}) custom-call(s32[1]{0:T(128)} %bitcast.me_ref, bf16[256,1024]{1,0:T(8,128)(2,1)S(1)} %copy-done, bf16[256,512]{1,0:T(8,128)(2,1)S(1)} %get-tuple-element.22.refs_1_, f32[8,256]{1,0:T(8,128)S(1)} %get-tuple-element.19.refs_2_.aux_ref, ...), custom_call_target="tpu_custom_call" | custom-call | flops 201326592 | bytes 1310720 | tf_op jit(solution)/shard_map/pallas_call | solution.py:205
  37.0 0.0 collective-permute-done.4.refs_7_
  37.0 0.0 collective-permute-done.3.refs_6_
  37.0 1.2 %shard_map.67 = (bf16[256,256]{1,0:T(8,128)(2,1)S(1)}, f32[8,256]{1,0:T(8,128)S(1)}) custom-call(s32[1]{0:T(128)} %bitcast.me_ref, bf16[256,1024]{1,0:T(8,128)(2,1)S(1)} %copy-done, bf16[256,512]{1,0:T(8,128)(2,1)S(1)} %get-tuple-element.18.refs_1_, f32[8,256]{1,0:T(8,128)S(1)} %get-tuple-element.19.refs_2_.aux_ref, ...), custom_call_target="tpu_custom_call" | custom-call | flops 201326592 | bytes 1310720 | tf_op jit(solution)/shard_map/pallas_call | solution.py:205
  38.2 0.0 copy-start.5
  38.2 2.4 %collective-permute-start.9 = (f32[8,256]{1,0:T(8,128)S(1)}, f32[8,256]{1,0:T(8,128)S(1)}, u32[]{:S(2)}, u32[]{:S(2)}) collective-permute-start(f32[8,256]{1,0:T(8,128)S(1)} %get-tuple-element.26.mine_ref), channel_id=1, source_target_pairs={{0,1},{1,0},{2,3},{3,2},{4,5},{5,4},{6,7},{7,6},{8,9},{9,8},{10,11... | collective-permute-start | bytes 24584 | tf_op jit(solution)/shard_map/ppermute | solution.py:222
  40.7 0.8 %collective-permute-done.9.other_ref = f32[8,256]{1,0:T(8,128)S(1)} collective-permute-done((f32[8,256]{1,0:T(8,128)S(1)}, f32[8,256]{1,0:T(8,128)S(1)}, u32[]{:S(2)}, u32[]{:S(2)}) %collective-permute-start.9) | collective-permute-done | bytes 8224 | tf_op jit(solution)/shard_map/ppermute | solution.py:222
  41.5 0.0 copy-done.5
  41.5 1.1 %finish.1 = bf16[256,1024]{1,0:T(8,128)(2,1)} custom-call(f32[8,256]{1,0:T(8,128)S(1)} %get-tuple-element.26.mine_ref, f32[8,256]{1,0:T(8,128)S(1)} %collective-permute-done.9.other_ref, f32[8,256]{1,0:T(8,128)S(1)} %get-tuple-element.19.refs_2_.aux_ref, f32[2,1024]{1,0:T(2,128)S(1)} %copy-done.5, bf16[256,256]{1,0:T(8,128)(2,1)S(1)} %get-tuple-element.27.refs_0_, ...), custom_call_target="tpu_custom_call" | custom-call | tf_op jit(solution)/shard_map/finish/pallas_call | solution.py:223
  (4 shorter events, 0.1 us)
Async XLA Ops:
  0.0 1.0 %copy-start.1 = (bf16[256,1024]{1,0:T(8,128)(2,1)S(1)}, bf16[256,1024]{1,0:T(8,128)(2,1)}, u32[]{:S(2)}) copy-start(bf16[256,1024]{1,0:T(8,128)(2,1)} %keys_ref.3) | copy-start | bytes 1572868
  1.0 1.0 %copy-start.3 = (bf16[256,1024]{1,0:T(8,128)(2,1)S(1)}, bf16[256,1024]{1,0:T(8,128)(2,1)}, u32[]{:S(2)}) copy-start(bf16[256,1024]{1,0:T(8,128)(2,1)} %values_ref.3) | copy-start | bytes 1572868
  2.1 5.1 %copy-start.2 = (bf16[256,1024]{1,0:T(8,128)(2,1)S(1)}, bf16[256,1024]{1,0:T(8,128)(2,1)}, u32[]{:S(2)}) copy-start(bf16[256,1024]{1,0:T(8,128)(2,1)} %keys_ref.3) | copy-start | bytes 1572868
  2.1 5.1 %copy-start.4 = (bf16[256,1024]{1,0:T(8,128)(2,1)S(1)}, bf16[256,1024]{1,0:T(8,128)(2,1)}, u32[]{:S(2)}) copy-start(bf16[256,1024]{1,0:T(8,128)(2,1)} %values_ref.3) | copy-start | bytes 1572868
  2.3 7.2 %collective-permute-start.7 = (bf16[256,512]{1,0:T(8,128)(2,1)S(1)}, bf16[256,512]{1,0:T(8,128)(2,1)S(1)}, u32[]{:S(2)}, u32[]{:S(2)}) collective-permute-start(bf16[256,512]{1,0:T(8,128)(2,1)S(1)} %get-tuple-element.24.refs_1_), channel_id=1, source_target_pairs={{0,4},{2,6},{4,8},{6,10},{8,12},{10,14},{12,0},{14,2},{1,5},{3,7},... | collective-permute-start | bytes 786440 | tf_op jit(solution)/shard_map/ppermute | solution.py:158
  3.6 11.5 %collective-permute-start.5 = (bf16[256,512]{1,0:T(8,128)(2,1)S(1)}, bf16[256,512]{1,0:T(8,128)(2,1)S(1)}, u32[]{:S(2)}, u32[]{:S(2)}) collective-permute-start(bf16[256,512]{1,0:T(8,128)(2,1)S(1)} %get-tuple-element.22.refs_1_), channel_id=1, source_target_pairs={{0,4},{2,6},{4,8},{6,10},{8,12},{10,14},{12,0},{14,2},{1,5},{3,7},... | collective-permute-start | bytes 786440 | tf_op jit(solution)/shard_map/ppermute | solution.py:158
  4.9 22.2 %collective-permute-start.2 = (bf16[256,512]{1,0:T(8,128)(2,1)S(1)}, bf16[256,512]{1,0:T(8,128)(2,1)S(1)}, u32[]{:S(2)}, u32[]{:S(2)}) collective-permute-start(bf16[256,512]{1,0:T(8,128)(2,1)S(1)} %get-tuple-element.18.refs_1_), channel_id=1, source_target_pairs={{0,2},{2,0},{4,6},{6,4},{8,10},{10,8},{12,14},{14,12},{1,3},{3,1},... | collective-permute-start | bytes 786440 | tf_op jit(solution)/shard_map/ppermute | solution.py:158
  5.2 31.8 %collective-permute-start.4 = (bf16[256,512]{1,0:T(8,128)(2,1)S(1)}, bf16[256,512]{1,0:T(8,128)(2,1)S(1)}, u32[]{:S(2)}, u32[]{:S(2)}) collective-permute-start(bf16[256,512]{1,0:T(8,128)(2,1)S(1)} %get-tuple-element.18.refs_1_), channel_id=1, source_target_pairs={{0,4},{2,6},{4,8},{6,10},{8,12},{10,14},{1,5},{3,7},{5,9},{7,11},{... | collective-permute-start | bytes 786440 | tf_op jit(solution)/shard_map/ppermute | solution.py:158
  7.1 0.7 %copy-start.7 = (s32[256]{0:T(256)S(1)}, s32[256]{0:T(256)}, u32[]{:S(2)}) copy-start(s32[256]{0:T(256)} %param.10) | copy-start | bytes 3076
  7.2 0.7 %copy-start.6 = (s32[256]{0:T(256)S(1)}, s32[256]{0:T(256)}, u32[]{:S(2)}) copy-start(s32[256]{0:T(256)} %param.9) | copy-start | bytes 3076
  7.9 18.8 %collective-permute-start = (bf16[272,512]{1,0:T(8,128)(2,1)S(1)}, bf16[272,512]{1,0:T(8,128)(2,1)S(1)}, u32[]{:S(2)}, u32[]{:S(2)}) collective-permute-start(bf16[272,512]{1,0:T(8,128)(2,1)S(1)} %get-tuple-element.20.refs_1_), channel_id=1, source_target_pairs={{0,4},{2,6},{4,8},{6,10},{8,12},{10,14},{12,0},{14,2},{1,5},{3,7},... | collective-permute-start | bytes 835592 | tf_op jit(solution)/shard_map/ppermute | solution.py:158
  9.5 25.1 %collective-permute-start.8 = (bf16[256,512]{1,0:T(8,128)(2,1)S(1)}, bf16[256,512]{1,0:T(8,128)(2,1)S(1)}, u32[]{:S(2)}, u32[]{:S(2)}) collective-permute-start(bf16[256,512]{1,0:T(8,128)(2,1)S(1)} %broadcast_select_fusion.1), channel_id=1, source_target_pairs={{0,2},{2,0},{4,6},{6,4},{8,10},{10,8},{12,14},{14,12},{1,3},{3,1},... | collective-permute-start | bytes 786440 | tf_op jit(solution)/shard_map/ppermute | solution.py:158
  15.2 20.7 %collective-permute-start.6 = (bf16[256,512]{1,0:T(8,128)(2,1)S(1)}, bf16[256,512]{1,0:T(8,128)(2,1)S(1)}, u32[]{:S(2)}, u32[]{:S(2)}) collective-permute-start(bf16[256,512]{1,0:T(8,128)(2,1)S(1)} %broadcast_select_fusion.2), channel_id=1, source_target_pairs={{0,2},{2,0},{4,6},{6,4},{8,10},{10,8},{12,14},{14,12},{1,3},{3,1},... | collective-permute-start | bytes 786440 | tf_op jit(solution)/shard_map/ppermute | solution.py:158
  26.7 6.8 %copy-start = (bf16[256,1024]{1,0:T(8,128)(2,1)S(1)}, bf16[256,1024]{1,0:T(8,128)(2,1)}, u32[]{:S(2)}) copy-start(bf16[256,1024]{1,0:T(8,128)(2,1)} %refs_0_.7) | copy-start | bytes 1572868
  26.8 6.8 %collective-permute-start.1 = (bf16[272,512]{1,0:T(8,128)(2,1)S(1)}, bf16[272,512]{1,0:T(8,128)(2,1)S(1)}, u32[]{:S(2)}, u32[]{:S(2)}) collective-permute-start(bf16[272,512]{1,0:T(8,128)(2,1)S(1)} %broadcast_select_fusion), channel_id=1, source_target_pairs={{0,2},{2,0},{4,6},{6,4},{8,10},{10,8},{12,14},{14,12},{1,3},{3,1},... | collective-permute-start | bytes 835592 | tf_op jit(solution)/shard_map/ppermute | solution.py:158
  27.1 9.9 %collective-permute-start.3 = (bf16[256,512]{1,0:T(8,128)(2,1)S(1)}, bf16[256,512]{1,0:T(8,128)(2,1)S(1)}, u32[]{:S(2)}, u32[]{:S(2)}) collective-permute-start(bf16[256,512]{1,0:T(8,128)(2,1)S(1)} %broadcast_select_fusion.3), channel_id=1, source_target_pairs={{0,4},{2,6},{4,8},{6,10},{8,12},{10,14},{12,0},{14,2},{1,5},{3,7},... | collective-permute-start | bytes 786440 | tf_op jit(solution)/shard_map/ppermute | solution.py:158
  38.2 3.3 %copy-start.5 = (f32[2,1024]{1,0:T(2,128)S(1)}, f32[2,1024]{1,0:T(2,128)}, u32[]{:S(2)}) copy-start(f32[2,1024]{1,0:T(2,128)} %gain_ref.1) | copy-start | bytes 24580
  38.2 3.3 %collective-permute-start.9 = (f32[8,256]{1,0:T(8,128)S(1)}, f32[8,256]{1,0:T(8,128)S(1)}, u32[]{:S(2)}, u32[]{:S(2)}) collective-permute-start(f32[8,256]{1,0:T(8,128)S(1)} %get-tuple-element.26.mine_ref), channel_id=1, source_target_pairs={{0,1},{1,0},{2,3},{3,2},{4,5},{5,4},{6,7},{7,6},{8,9},{9,8},{10,11... | collective-permute-start | bytes 24584 | tf_op jit(solution)/shard_map/ppermute | solution.py:222

commit v3 on v2

--- a/solution.py
+++ b/solution.py
@@ -14,6 +14,7 @@
 SEG_ROWS = 16
 NEG = -1e30
 EPS = 1e-05
+FINISH_BLOCKS = 4
 VMEM_LIMIT = 12 * 1024 * 1024
 
 
@@ -131,17 +132,26 @@
 
 
 def finish_kernel(features, mine_ref, other_ref, aux_ref, gain_ref, *refs):
-    att_refs, out_ref = refs[:-1], refs[-1]
+    att_refs, (out_hbm, out_ref, sem) = refs[:-3], refs[-3:]
+    tok = out_ref.shape[0]
     total = jnp.sum(mine_ref[...] + other_ref[...], axis=0, keepdims=True)
     inverse = column(lax.rsqrt(total / features + EPS))
     image = column(aux_ref[1:2, :]) == 1.0
-    for c, att_ref in enumerate(att_refs):
-        width = att_ref.shape[1]
-        for b in range(width // 128):
-            at = c * width + b * 128
-            gain = jnp.where(image, gain_ref[1:2, at : at + 128], gain_ref[0:1, at : at + 128])
-            att = att_ref[:, b * 128 : (b + 1) * 128].astype(jnp.float32)
-            out_ref[:, at : at + 128] = (att * inverse * gain).astype(jnp.bfloat16)
+    rows = tok // FINISH_BLOCKS
+    copies = []
+    for r in range(FINISH_BLOCKS):
+        block = slice(r * rows, (r + 1) * rows)
+        for c, att_ref in enumerate(att_refs):
+            width = att_ref.shape[1]
+            for b in range(width // 128):
+                at = c * width + b * 128
+                gain = jnp.where(image[block], gain_ref[1:2, at : at + 128], gain_ref[0:1, at : at + 128])
+                att = att_ref[block, b * 128 : (b + 1) * 128].astype(jnp.float32)
+                out_ref[block, at : at + 128] = (att * inverse[block] * gain).astype(jnp.bfloat16)
+        copies.append(pltpu.make_async_copy(out_ref.at[block], out_hbm.at[block], sem.at[r]))
+        copies[-1].start()
+    for copy in copies:
+        copy.wait()
 
 
 def on_device(queries, keys, values, segment_ids, modality, norm_gain):
@@ -163,6 +173,7 @@
     smem = pl.BlockSpec(memory_space=pltpu.SMEM)
     vmem = pl.BlockSpec(memory_space=pltpu.VMEM)
     hbm = pl.BlockSpec(memory_space=pltpu.HBM)
+    in_hbm = lambda a: pltpu.with_memory_space_constraint(a, pltpu.HBM)
     small = pltpu.CompilerParams(vmem_limit_bytes=VMEM_LIMIT)
     me1 = me.astype(jnp.int32)[None]
     first, aux = pl.pallas_call(
@@ -176,7 +187,7 @@
         scratch_shapes=[pltpu.VMEM((2, 1, tok), jnp.int32), pltpu.SemaphoreType.DMA((4,))],
         name="pack",
         compiler_params=small,
-    )(me1, keys, values, segment_ids[None, :], modality[None, :])
+    )(me1, in_hbm(keys), in_hbm(values), in_hbm(segment_ids[None, :]), in_hbm(modality[None, :]))
     rest = pl.pallas_call(
         pack_rest_kernel,
         out_shape=tuple(jax.ShapeDtypeStruct((tok, 2 * width), jnp.bfloat16) for _ in range(CHUNKS - 1)),
@@ -185,7 +196,7 @@
         scratch_shapes=[pltpu.SemaphoreType.DMA((2 * CHUNKS - 2,))],
         name="pack_rest",
         compiler_params=small,
-    )(keys, values)
+    )(in_hbm(keys), in_hbm(values))
     chunk = (first, *rest)
     a0 = send(chunk[0], ring2)
     s = send(chunk[3], pair)
@@ -224,7 +235,8 @@
         functools.partial(finish_kernel, float(feat * tp)),
         out_shape=jax.ShapeDtypeStruct((tok, feat), jnp.bfloat16),
         in_specs=[vmem] * (4 + CHUNKS),
-        out_specs=vmem,
+        out_specs=hbm,
+        scratch_shapes=[pltpu.VMEM((tok, feat), jnp.bfloat16), pltpu.SemaphoreType.DMA((FINISH_BLOCKS,))],
         name="finish",
         compiler_params=small,
     )(q, other, aux, norm_gain, *att)

time: 43.3 us -> 42.2 us (0.975)
  local copies, waits for them, and re-layouts: 2.76 us -> 0.01 us
  Pallas kernels: 5.98 us -> 8 us
  waiting for transfers between devices: 22.1 us -> 21.6 us
    unnamed x16 -> x4, local copies, waits for them, and re-layouts: 2.76 us -> 0.01 us
    pallas_call x1, Pallas kernels: 0.17 us -> 1.26 us  [on_device(): pl.pallas_call(pack_rest_kernel, out_shape=tuple((jax.ShapeDtypeStruct((t...]
    pallas_call x1, Pallas kernels: 0.08 us -> 1.04 us  [on_device(): pl.pallas_call(pack_kernel, out_shape=(jax.ShapeDtypeStruct((tok + SEG_RO...]
    ppermute x9, waiting for transfers between devices: 21.3 us -> 20.8 us  [send(): return lax.ppermute(value, 'seq', pairs)]
  transfers between devices with their start and end apart: 10 -> 10, of which waited for: 5 -> 5; matrix products, arithmetic and copies ran while one was open for 0% -> 0% of each run, Pallas kernels for 8% -> 11%
where the time goes in v3:
time: 42.2 us; the launch traced here: 41.6 us
  waiting for transfers between devices  21.6 us (51%)
  starting transfers between devices  11.7 us (28%)
  Pallas kernels  8 us (19%)
    ppermute x9, waiting for transfers between devices, send(): return lax.ppermute(value, 'seq', pairs)  20.8 us
    ppermute x9, starting transfers between devices, send(): return lax.ppermute(value, 'seq', pairs)  9.26 us
    pallas_call x4, Pallas kernels, attend(): pl.pallas_call(functools.partial(attend_kernel, c, last), out_shape=outs,...  4.66 us
    ppermute x1, starting transfers between devices, on_device(): other = lax.ppermute(q, 'tp', [(i, i ^ 1) for i in range(tp)])  2.45 us
    pallas_call x1, Pallas kernels, on_device(): pl.pallas_call(pack_rest_kernel, out_shape=tuple((jax.ShapeDtypeStruct((t...  1.26 us
    pallas_call x1, Pallas kernels, on_device(): pl.pallas_call(pack_kernel, out_shape=(jax.ShapeDtypeStruct((tok + SEG_RO...  1.04 us
    pallas_call x1, Pallas kernels, on_device(): pl.pallas_call(functools.partial(finish_kernel, float(feat * tp)), out_sh...  1.04 us
  transfers between devices with their start and end apart: 10, of which 5 were waited for; matrix products, arithmetic and copies ran while one was open for 0% of the time, Pallas kernels for 11%

profile of v3, /device:TPU:11, one launch (start us, length us, event | category | flops | bytes accessed | tf_op | source)
XLA Modules:
  0.0 41.6 jit_solution(17184940611798004814)
XLA Ops:
  0.0 1.3 %pack_rest.1 = (bf16[256,512]{1,0:T(8,128)(2,1)S(1)}, bf16[256,512]{1,0:T(8,128)(2,1)S(1)}, bf16[256,512]{1,0:T(8,128)(2,1)S(1)}) custom-call(bf16[256,1024]{1,0:T(8,128)(2,1)} %keys_ref.3, bf16[256,1024]{1,0:T(8,128)(2,1)} %values_ref.3), custom_call_target="tpu_custom_call" | custom-call | tf_op jit(solution)/shard_map/pack_rest/pallas_call | solution.py:191
  1.3 1.3 %collective-permute-start.7 = (bf16[256,512]{1,0:T(8,128)(2,1)S(1)}, bf16[256,512]{1,0:T(8,128)(2,1)S(1)}, u32[]{:S(2)}, u32[]{:S(2)}) collective-permute-start(bf16[256,512]{1,0:T(8,128)(2,1)S(1)} %get-tuple-element.24.refs_1_), channel_id=1, source_target_pairs={{0,4},{2,6},{4,8},{6,10},{8,12},{10,14},{12,0},{14,2},{1,5},{3,7},... | collective-permute-start | bytes 786440 | tf_op jit(solution)/shard_map/ppermute | solution.py:168
  2.6 1.3 %collective-permute-start.5 = (bf16[256,512]{1,0:T(8,128)(2,1)S(1)}, bf16[256,512]{1,0:T(8,128)(2,1)S(1)}, u32[]{:S(2)}, u32[]{:S(2)}) collective-permute-start(bf16[256,512]{1,0:T(8,128)(2,1)S(1)} %get-tuple-element.22.refs_1_), channel_id=1, source_target_pairs={{0,4},{2,6},{4,8},{6,10},{8,12},{10,14},{12,0},{14,2},{1,5},{3,7},... | collective-permute-start | bytes 786440 | tf_op jit(solution)/shard_map/ppermute | solution.py:168
  3.9 0.3 collective-permute-start.2
  4.2 2.0 %collective-permute-start.4 = (bf16[256,512]{1,0:T(8,128)(2,1)S(1)}, bf16[256,512]{1,0:T(8,128)(2,1)S(1)}, u32[]{:S(2)}, u32[]{:S(2)}) collective-permute-start(bf16[256,512]{1,0:T(8,128)(2,1)S(1)} %get-tuple-element.18.refs_1_), channel_id=1, source_target_pairs={{0,4},{2,6},{4,8},{6,10},{8,12},{10,14},{1,5},{3,7},{5,9},{7,11},{... | collective-permute-start | bytes 786440 | tf_op jit(solution)/shard_map/ppermute | solution.py:168
  6.1 1.0 %pack.1 = (bf16[272,512]{1,0:T(8,128)(2,1)S(1)}, f32[8,256]{1,0:T(8,128)S(1)}) custom-call(s32[1]{0:T(128)} %bitcast.me_ref, bf16[256,1024]{1,0:T(8,128)(2,1)} %keys_ref.3, bf16[256,1024]{1,0:T(8,128)(2,1)} %values_ref.3, s32[1,256]{1,0:T(1,128)} %bitcast.3, s32[1,256]{1,0:T(1,128)} %bitcast.4), custom_call_target="tpu_custom_call" | custom-call | tf_op jit(solution)/shard_map/pack/pallas_call | solution.py:179
  7.2 1.2 %collective-permute-start = (bf16[272,512]{1,0:T(8,128)(2,1)S(1)}, bf16[272,512]{1,0:T(8,128)(2,1)S(1)}, u32[]{:S(2)}, u32[]{:S(2)}) collective-permute-start(bf16[272,512]{1,0:T(8,128)(2,1)S(1)} %get-tuple-element.20.refs_1_), channel_id=1, source_target_pairs={{0,4},{2,6},{4,8},{6,10},{8,12},{10,14},{12,0},{14,2},{1,5},{3,7},... | collective-permute-start | bytes 835592 | tf_op jit(solution)/shard_map/ppermute | solution.py:168
  8.4 0.1 collective-permute-done.7.refs_6_
  8.5 1.2 %collective-permute-start.8 = (bf16[256,512]{1,0:T(8,128)(2,1)S(1)}, bf16[256,512]{1,0:T(8,128)(2,1)S(1)}, u32[]{:S(2)}, u32[]{:S(2)}) collective-permute-start(bf16[256,512]{1,0:T(8,128)(2,1)S(1)} %broadcast_select_fusion.1), channel_id=1, source_target_pairs={{0,2},{2,0},{4,6},{6,4},{8,10},{10,8},{12,14},{14,12},{1,3},{3,1},... | collective-permute-start | bytes 786440 | tf_op jit(solution)/shard_map/ppermute | solution.py:168
  9.7 4.4 %collective-permute-done.5.refs_6_ = bf16[256,512]{1,0:T(8,128)(2,1)S(1)} collective-permute-done((bf16[256,512]{1,0:T(8,128)(2,1)S(1)}, bf16[256,512]{1,0:T(8,128)(2,1)S(1)}, u32[]{:S(2)}, u32[]{:S(2)}) %collective-permute-start.5) | collective-permute-done | bytes 262176 | tf_op jit(solution)/shard_map/ppermute | solution.py:168
  14.2 0.3 collective-permute-start.6
  14.5 11.2 %collective-permute-done.refs_4_.refs_6_ = bf16[272,512]{1,0:T(8,128)(2,1)S(1)} collective-permute-done((bf16[272,512]{1,0:T(8,128)(2,1)S(1)}, bf16[272,512]{1,0:T(8,128)(2,1)S(1)}, u32[]{:S(2)}, u32[]{:S(2)}) %collective-permute-start) | collective-permute-done | bytes 278560 | tf_op jit(solution)/shard_map/ppermute | solution.py:168
  25.8 0.0 copy-start
  25.8 0.3 collective-permute-start.1
  26.1 0.0 collective-permute-done.2.refs_5_
  26.1 1.3 %collective-permute-start.3 = (bf16[256,512]{1,0:T(8,128)(2,1)S(1)}, bf16[256,512]{1,0:T(8,128)(2,1)S(1)}, u32[]{:S(2)}, u32[]{:S(2)}) collective-permute-start(bf16[256,512]{1,0:T(8,128)(2,1)S(1)} %broadcast_select_fusion.3), channel_id=1, source_target_pairs={{0,4},{2,6},{4,8},{6,10},{8,12},{10,14},{12,0},{14,2},{1,5},{3,7},... | collective-permute-start | bytes 786440 | tf_op jit(solution)/shard_map/ppermute | solution.py:168
  27.5 5.0 %collective-permute-done.1.refs_3_.refs_5_ = bf16[272,512]{1,0:T(8,128)(2,1)S(1)} collective-permute-done((bf16[272,512]{1,0:T(8,128)(2,1)S(1)}, bf16[272,512]{1,0:T(8,128)(2,1)S(1)}, u32[]{:S(2)}, u32[]{:S(2)}) %collective-permute-start.1) | collective-permute-done | bytes 278560 | tf_op jit(solution)/shard_map/ppermute | solution.py:168
  32.5 0.0 copy-done
  32.5 1.1 %shard_map.64 = (bf16[256,256]{1,0:T(8,128)(2,1)S(1)}, f32[256,128]{1,0:T(8,128)S(1)}) custom-call(s32[1]{0:T(128)} %bitcast.me_ref, bf16[256,1024]{1,0:T(8,128)(2,1)S(1)} %copy-done, bf16[272,512]{1,0:T(8,128)(2,1)S(1)} %get-tuple-element.20.refs_1_, f32[8,256]{1,0:T(8,128)S(1)} %get-tuple-element.19.refs_2_.aux_ref, ...), custom_call_target="tpu_custom_call" | custom-call | flops 201326592 | bytes 1310720 | tf_op jit(solution)/shard_map/pallas_call | solution.py:216
  33.7 0.0 collective-permute-done.8.refs_5_
  33.7 1.1 %shard_map.66 = (bf16[256,256]{1,0:T(8,128)(2,1)S(1)}, f32[256,128]{1,0:T(8,128)S(1)}) custom-call(s32[1]{0:T(128)} %bitcast.me_ref, bf16[256,1024]{1,0:T(8,128)(2,1)S(1)} %copy-done, bf16[256,512]{1,0:T(8,128)(2,1)S(1)} %get-tuple-element.24.refs_1_, f32[8,256]{1,0:T(8,128)S(1)} %get-tuple-element.19.refs_2_.aux_ref, ...), custom_call_target="tpu_custom_call" | custom-call | flops 201326592 | bytes 1310720 | tf_op jit(solution)/shard_map/pallas_call | solution.py:216
  34.8 0.0 collective-permute-done.6.refs_5_
  34.8 1.1 %shard_map.65 = (bf16[256,256]{1,0:T(8,128)(2,1)S(1)}, f32[256,128]{1,0:T(8,128)S(1)}) custom-call(s32[1]{0:T(128)} %bitcast.me_ref, bf16[256,1024]{1,0:T(8,128)(2,1)S(1)} %copy-done, bf16[256,512]{1,0:T(8,128)(2,1)S(1)} %get-tuple-element.22.refs_1_, f32[8,256]{1,0:T(8,128)S(1)} %get-tuple-element.19.refs_2_.aux_ref, ...), custom_call_target="tpu_custom_call" | custom-call | flops 201326592 | bytes 1310720 | tf_op jit(solution)/shard_map/pallas_call | solution.py:216
  36.0 0.0 collective-permute-done.4.refs_7_
  36.0 0.0 collective-permute-done.3.refs_6_
  36.0 1.2 %shard_map.67 = (bf16[256,256]{1,0:T(8,128)(2,1)S(1)}, f32[8,256]{1,0:T(8,128)S(1)}) custom-call(s32[1]{0:T(128)} %bitcast.me_ref, bf16[256,1024]{1,0:T(8,128)(2,1)S(1)} %copy-done, bf16[256,512]{1,0:T(8,128)(2,1)S(1)} %get-tuple-element.18.refs_1_, f32[8,256]{1,0:T(8,128)S(1)} %get-tuple-element.19.refs_2_.aux_ref, ...), custom_call_target="tpu_custom_call" | custom-call | flops 201326592 | bytes 1310720 | tf_op jit(solution)/shard_map/pallas_call | solution.py:216
  37.2 0.0 copy-start.1
  37.2 2.4 %collective-permute-start.9 = (f32[8,256]{1,0:T(8,128)S(1)}, f32[8,256]{1,0:T(8,128)S(1)}, u32[]{:S(2)}, u32[]{:S(2)}) collective-permute-start(f32[8,256]{1,0:T(8,128)S(1)} %get-tuple-element.26.mine_ref), channel_id=1, source_target_pairs={{0,1},{1,0},{2,3},{3,2},{4,5},{5,4},{6,7},{7,6},{8,9},{9,8},{10,11... | collective-permute-start | bytes 24584 | tf_op jit(solution)/shard_map/ppermute | solution.py:233
  39.7 0.8 %collective-permute-done.9.other_ref = f32[8,256]{1,0:T(8,128)S(1)} collective-permute-done((f32[8,256]{1,0:T(8,128)S(1)}, f32[8,256]{1,0:T(8,128)S(1)}, u32[]{:S(2)}, u32[]{:S(2)}) %collective-permute-start.9) | collective-permute-done | bytes 8224 | tf_op jit(solution)/shard_map/ppermute | solution.py:233
  40.5 0.0 copy-done.1
  40.5 1.0 %finish.1 = bf16[256,1024]{1,0:T(8,128)(2,1)} custom-call(f32[8,256]{1,0:T(8,128)S(1)} %get-tuple-element.26.mine_ref, f32[8,256]{1,0:T(8,128)S(1)} %collective-permute-done.9.other_ref, f32[8,256]{1,0:T(8,128)S(1)} %get-tuple-element.19.refs_2_.aux_ref, f32[2,1024]{1,0:T(2,128)S(1)} %copy-done.1, bf16[256,256]{1,0:T(8,128)(2,1)S(1)} %get-tuple-element.27.refs_0_, ...), custom_call_target="tpu_custom_call" | custom-call | tf_op jit(solution)/shard_map/finish/pallas_call | solution.py:234
  (4 shorter events, 0.1 us)
Async XLA Ops:
  1.3 7.2 %collective-permute-start.7 = (bf16[256,512]{1,0:T(8,128)(2,1)S(1)}, bf16[256,512]{1,0:T(8,128)(2,1)S(1)}, u32[]{:S(2)}, u32[]{:S(2)}) collective-permute-start(bf16[256,512]{1,0:T(8,128)(2,1)S(1)} %get-tuple-element.24.refs_1_), channel_id=1, source_target_pairs={{0,4},{2,6},{4,8},{6,10},{8,12},{10,14},{12,0},{14,2},{1,5},{3,7},... | collective-permute-start | bytes 786440 | tf_op jit(solution)/shard_map/ppermute | solution.py:168
  2.6 11.5 %collective-permute-start.5 = (bf16[256,512]{1,0:T(8,128)(2,1)S(1)}, bf16[256,512]{1,0:T(8,128)(2,1)S(1)}, u32[]{:S(2)}, u32[]{:S(2)}) collective-permute-start(bf16[256,512]{1,0:T(8,128)(2,1)S(1)} %get-tuple-element.22.refs_1_), channel_id=1, source_target_pairs={{0,4},{2,6},{4,8},{6,10},{8,12},{10,14},{12,0},{14,2},{1,5},{3,7},... | collective-permute-start | bytes 786440 | tf_op jit(solution)/shard_map/ppermute | solution.py:168
  3.9 22.2 %collective-permute-start.2 = (bf16[256,512]{1,0:T(8,128)(2,1)S(1)}, bf16[256,512]{1,0:T(8,128)(2,1)S(1)}, u32[]{:S(2)}, u32[]{:S(2)}) collective-permute-start(bf16[256,512]{1,0:T(8,128)(2,1)S(1)} %get-tuple-element.18.refs_1_), channel_id=1, source_target_pairs={{0,2},{2,0},{4,6},{6,4},{8,10},{10,8},{12,14},{14,12},{1,3},{3,1},... | collective-permute-start | bytes 786440 | tf_op jit(solution)/shard_map/ppermute | solution.py:168
  4.2 31.8 %collective-permute-start.4 = (bf16[256,512]{1,0:T(8,128)(2,1)S(1)}, bf16[256,512]{1,0:T(8,128)(2,1)S(1)}, u32[]{:S(2)}, u32[]{:S(2)}) collective-permute-start(bf16[256,512]{1,0:T(8,128)(2,1)S(1)} %get-tuple-element.18.refs_1_), channel_id=1, source_target_pairs={{0,4},{2,6},{4,8},{6,10},{8,12},{10,14},{1,5},{3,7},{5,9},{7,11},{... | collective-permute-start | bytes 786440 | tf_op jit(solution)/shard_map/ppermute | solution.py:168
  7.2 18.5 %collective-permute-start = (bf16[272,512]{1,0:T(8,128)(2,1)S(1)}, bf16[272,512]{1,0:T(8,128)(2,1)S(1)}, u32[]{:S(2)}, u32[]{:S(2)}) collective-permute-start(bf16[272,512]{1,0:T(8,128)(2,1)S(1)} %get-tuple-element.20.refs_1_), channel_id=1, source_target_pairs={{0,4},{2,6},{4,8},{6,10},{8,12},{10,14},{12,0},{14,2},{1,5},{3,7},... | collective-permute-start | bytes 835592 | tf_op jit(solution)/shard_map/ppermute | solution.py:168
  8.5 25.1 %collective-permute-start.8 = (bf16[256,512]{1,0:T(8,128)(2,1)S(1)}, bf16[256,512]{1,0:T(8,128)(2,1)S(1)}, u32[]{:S(2)}, u32[]{:S(2)}) collective-permute-start(bf16[256,512]{1,0:T(8,128)(2,1)S(1)} %broadcast_select_fusion.1), channel_id=1, source_target_pairs={{0,2},{2,0},{4,6},{6,4},{8,10},{10,8},{12,14},{14,12},{1,3},{3,1},... | collective-permute-start | bytes 786440 | tf_op jit(solution)/shard_map/ppermute | solution.py:168
  14.2 20.7 %collective-permute-start.6 = (bf16[256,512]{1,0:T(8,128)(2,1)S(1)}, bf16[256,512]{1,0:T(8,128)(2,1)S(1)}, u32[]{:S(2)}, u32[]{:S(2)}) collective-permute-start(bf16[256,512]{1,0:T(8,128)(2,1)S(1)} %broadcast_select_fusion.2), channel_id=1, source_target_pairs={{0,2},{2,0},{4,6},{6,4},{8,10},{10,8},{12,14},{14,12},{1,3},{3,1},... | collective-permute-start | bytes 786440 | tf_op jit(solution)/shard_map/ppermute | solution.py:168
  25.8 6.8 %copy-start = (bf16[256,1024]{1,0:T(8,128)(2,1)S(1)}, bf16[256,1024]{1,0:T(8,128)(2,1)}, u32[]{:S(2)}) copy-start(bf16[256,1024]{1,0:T(8,128)(2,1)} %refs_0_.7) | copy-start | bytes 1572868
  25.8 6.8 %collective-permute-start.1 = (bf16[272,512]{1,0:T(8,128)(2,1)S(1)}, bf16[272,512]{1,0:T(8,128)(2,1)S(1)}, u32[]{:S(2)}, u32[]{:S(2)}) collective-permute-start(bf16[272,512]{1,0:T(8,128)(2,1)S(1)} %broadcast_select_fusion), channel_id=1, source_target_pairs={{0,2},{2,0},{4,6},{6,4},{8,10},{10,8},{12,14},{14,12},{1,3},{3,1},... | collective-permute-start | bytes 835592 | tf_op jit(solution)/shard_map/ppermute | solution.py:168
  26.1 9.9 %collective-permute-start.3 = (bf16[256,512]{1,0:T(8,128)(2,1)S(1)}, bf16[256,512]{1,0:T(8,128)(2,1)S(1)}, u32[]{:S(2)}, u32[]{:S(2)}) collective-permute-start(bf16[256,512]{1,0:T(8,128)(2,1)S(1)} %broadcast_select_fusion.3), channel_id=1, source_target_pairs={{0,4},{2,6},{4,8},{6,10},{8,12},{10,14},{12,0},{14,2},{1,5},{3,7},... | collective-permute-start | bytes 786440 | tf_op jit(solution)/shard_map/ppermute | solution.py:168
  37.2 3.3 %copy-start.1 = (f32[2,1024]{1,0:T(2,128)S(1)}, f32[2,1024]{1,0:T(2,128)}, u32[]{:S(2)}) copy-start(f32[2,1024]{1,0:T(2,128)} %gain_ref.1) | copy-start | bytes 24580
  37.2 3.3 %collective-permute-start.9 = (f32[8,256]{1,0:T(8,128)S(1)}, f32[8,256]{1,0:T(8,128)S(1)}, u32[]{:S(2)}, u32[]{:S(2)}) collective-permute-start(f32[8,256]{1,0:T(8,128)S(1)} %get-tuple-element.26.mine_ref), channel_id=1, source_target_pairs={{0,1},{1,0},{2,3},{3,2},{4,5},{5,4},{6,7},{7,6},{8,9},{9,8},{10,11... | collective-permute-start | bytes 24584 | tf_op jit(solution)/shard_map/ppermute | solution.py:233

commit v4 on v3

--- a/solution.py
+++ b/solution.py
@@ -11,6 +11,7 @@
 
 HEAD_DIM = 128
 CHUNKS = 4
+FACTOR = HEAD_DIM ** (-0.5) * math.log2(math.e)
 SEG_ROWS = 16
 NEG = -1e30
 EPS = 1e-05
@@ -37,21 +38,38 @@
     return own, q_seg == near_seg, q_seg == far_seg
 
 
-def attend_head(q, keys, values, masks):
-    factor = HEAD_DIM ** (-0.5) * math.log2(math.e)
+def own_mask(own_seg):
+    tok = own_seg.shape[1]
+    q_pos = lax.broadcasted_iota(jnp.int32, (tok, tok), 0)
+    k_pos = lax.broadcasted_iota(jnp.int32, (tok, tok), 1)
+    return (lanes(column(own_seg), tok) == own_seg) & (k_pos <= q_pos)
+
+
+def weigh(q, keys, masks):
     scores = []
     for key, mask in zip(keys, masks):
         s = lax.dot_general(q, key, (((1,), (1,)), ((), ())), preferred_element_type=jnp.float32)
         scores.append(jnp.where(mask, s, NEG))
     top = functools.reduce(jnp.maximum, scores)
-    top = jnp.max(top, axis=1, keepdims=True) * factor
-    weights = [jnp.exp2(s * factor - top) for s in scores]
+    top = jnp.max(top, axis=1, keepdims=True) * FACTOR
+    weights = [jnp.exp2(s * FACTOR - top) for s in scores]
     total = jnp.sum(functools.reduce(jnp.add, weights), axis=1, keepdims=True)
-    acc = sum(
+    return weights, top, total
+
+
+def gather(weights, values):
+    return sum(
         lax.dot_general(w.astype(jnp.bfloat16), v, (((1,), (0,)), ((), ())), preferred_element_type=jnp.float32)
         for w, v in zip(weights, values)
     )
-    return (acc / total).astype(jnp.bfloat16)
+
+
+def seg_of(ref, tok):
+    return ref[tok : tok + SEG_ROWS, :tok][0:1, :].astype(jnp.float32)
+
+
+def columns(width, h):
+    return slice(h * HEAD_DIM, (h + 1) * HEAD_DIM), slice(width + h * HEAD_DIM, width + (h + 1) * HEAD_DIM)
 
 
 def pack_kernel(me_ref, keys_ref, values_ref, seg_ref, mod_ref, chunk_ref, aux_ref, ids_ref, sem):
@@ -93,42 +111,99 @@
         copy.wait()
 
 
-def attend_kernel(c, last, me_ref, *refs):
-    q_ref, own_ref, aux_ref, near_seg_ref, far_seg_ref = refs[:5]
+def attend_kernel(c, me_ref, q_ref, own_ref, aux_ref, near_seg_ref, far_seg_ref, near_ref, far_ref, att_ref, sq_ref):
     me = me_ref[0]
     tok, width = q_ref.shape[0], q_ref.shape[1] // CHUNKS
-    near_seg = near_seg_ref[tok : tok + SEG_ROWS, :tok][0:1, :].astype(jnp.float32)
-    far_seg = far_seg_ref[tok : tok + SEG_ROWS, :tok][0:1, :].astype(jnp.float32)
-    masks = allowed_masks(me, aux_ref[0:1, :], near_seg, far_seg)
-    if last:
-        s_ref, f_ref, a_ref, p0, p1, p2 = refs[5:11]
-        att_ref, sq_ref = refs[11:]
-        odd = lax.rem(me, 2) == 1
-        near = jnp.where(odd, s_ref[...], f_ref[...])
-        far = jnp.where(odd, f_ref[...], a_ref[...])
-    else:
-        near_ref, far_ref = refs[5:7]
-        att_ref, sq_ref = refs[7:]
-        near, far = near_ref[:tok, :], far_ref[:tok, :]
-    squares = None
-    for h in range(width // HEAD_DIM):
-        ks = slice(h * HEAD_DIM, (h + 1) * HEAD_DIM)
-        vs = slice(width + h * HEAD_DIM, width + (h + 1) * HEAD_DIM)
-        own = slice(c * width + h * HEAD_DIM, c * width + (h + 1) * HEAD_DIM)
-        att = attend_head(
-            q_ref[:, own],
-            (own_ref[:tok, ks], near[:, ks], far[:, ks]),
-            (own_ref[:tok, vs], near[:, vs], far[:, vs]),
-            masks,
-        )
-        att_ref[:, ks] = att
-        att = att.astype(jnp.float32)
-        squares = att * att if squares is None else squares + att * att
-    if last:
-        squares = jnp.transpose(squares + p0[...] + p1[...] + p2[...])
+
+    def attend(blocks, masks):
+        squares = None
+        for h in range(width // HEAD_DIM):
+            ks, vs = columns(width, h)
+            q = q_ref[:, c * width + h * HEAD_DIM : c * width + (h + 1) * HEAD_DIM]
+            weights, _, total = weigh(q, [b[0:tok, ks] for b in blocks], masks)
+            att = (gather(weights, [b[0:tok, vs] for b in blocks]) / total).astype(jnp.bfloat16)
+            att_ref[:, ks] = att
+            att = att.astype(jnp.float32)
+            squares = att * att if squares is None else squares + att * att
+        sq_ref[...] = squares
+
+    @pl.when(me == 0)
+    def _():
+        attend([own_ref], [own_mask(aux_ref[0:1, :])])
+
+    @pl.when(me > 0)
+    def _():
+        masks = allowed_masks(me, aux_ref[0:1, :], seg_of(near_seg_ref, tok), seg_of(far_seg_ref, tok))
+        attend([own_ref, near_ref, far_ref], masks)
+
+
+def partial_kernel(c, me_ref, q_ref, own_ref, aux_ref, near_seg_ref, far_seg_ref, s_ref, f_ref, acc_ref, stat_ref):
+    me = me_ref[0]
+    odd = lax.rem(me, 2) == 1
+    tok, width = q_ref.shape[0], q_ref.shape[1] // CHUNKS
+
+    def attend(blocks, masks):
+        for h in range(width // HEAD_DIM):
+            ks, vs = columns(width, h)
+            q = q_ref[:, c * width + h * HEAD_DIM : c * width + (h + 1) * HEAD_DIM]
+            weights, top, total = weigh(q, [b[0:tok, ks] for b in blocks], masks)
+            acc_ref[:, ks] = gather(weights, [b[0:tok, vs] for b in blocks])
+            stat_ref[2 * h] = jnp.broadcast_to(top, (tok, HEAD_DIM))
+            stat_ref[2 * h + 1] = jnp.broadcast_to(total, (tok, HEAD_DIM))
+
+    @pl.when(me == 0)
+    def _():
+        attend([own_ref], [own_mask(aux_ref[0:1, :])])
+
+    @pl.when(me > 0)
+    def _():
+        masks = allowed_masks(me, aux_ref[0:1, :], seg_of(near_seg_ref, tok), seg_of(far_seg_ref, tok))
+
+        @pl.when(odd)
+        def _():
+            attend([own_ref, s_ref, f_ref], masks)
+
+        @pl.when(jnp.logical_not(odd))
+        def _():
+            attend([own_ref, f_ref], masks[:2])
+
+
+def last_kernel(c, me_ref, q_ref, aux_ref, far_seg_ref, far_ref, acc_ref, stat_ref, p0, p1, p2, att_ref, sq_ref):
+    me = me_ref[0]
+    tok, width = q_ref.shape[0], q_ref.shape[1] // CHUNKS
+    per = width // HEAD_DIM
+    merge = jnp.logical_and(lax.rem(me, 2) == 0, me >= 2)
+
+    def finish(parts):
+        squares = p0[...] + p1[...] + p2[...]
+        for h, att in enumerate(parts):
+            att = att.astype(jnp.bfloat16)
+            att_ref[:, columns(width, h)[0]] = att
+            att = att.astype(jnp.float32)
+            squares = squares + att * att
+        squares = jnp.transpose(squares)
         sq_ref[...] = jnp.sum(squares.reshape(squares.shape[0] // 8, 8, tok), axis=0)
-    else:
-        sq_ref[...] = squares
+
+    @pl.when(jnp.logical_not(merge))
+    def _():
+        finish([acc_ref[:, columns(width, h)[0]] / stat_ref[2 * h + 1] for h in range(per)])
+
+    @pl.when(merge)
+    def _():
+        mask = lanes(column(aux_ref[0:1, :]), tok) == seg_of(far_seg_ref, tok)
+        parts = []
+        for h in range(per):
+            ks, vs = columns(width, h)
+            q = q_ref[:, c * width + h * HEAD_DIM : c * width + (h + 1) * HEAD_DIM]
+            s = lax.dot_general(q, far_ref[:, ks], (((1,), (1,)), ((), ())), preferred_element_type=jnp.float32)
+            s = jnp.where(mask, s, NEG) * FACTOR
+            old = stat_ref[2 * h]
+            top = jnp.maximum(old, jnp.max(s, axis=1, keepdims=True))
+            weights = jnp.exp2(s - lanes(top, tok))
+            scale = jnp.exp2(old - top)
+            total = stat_ref[2 * h + 1] * scale + jnp.sum(weights, axis=1, keepdims=True)
+            parts.append((acc_ref[:, ks] * scale + gather([weights], [far_ref[:, vs]])) / total)
+        finish(parts)
 
 
 def finish_kernel(features, mine_ref, other_ref, aux_ref, gain_ref, *refs):
@@ -210,24 +285,31 @@
 
     flops = 3 * 4 * tok * tok * width
 
-    def attend(c, last, rest):
-        sq_shape = (8, tok) if last else (tok, 128)
-        outs = (jax.ShapeDtypeStruct((tok, width), jnp.bfloat16), jax.ShapeDtypeStruct(sq_shape, jnp.float32))
+    cost = pl.CostEstimate(flops=flops, bytes_accessed=tok * width * 20, transcendentals=3 * tok * tok * 2)
+    att_shape = jax.ShapeDtypeStruct((tok, width), jnp.bfloat16)
+    acc_shape = jax.ShapeDtypeStruct((tok, width), jnp.float32)
+    stat_shape = jax.ShapeDtypeStruct((2 * (width // HEAD_DIM), tok, HEAD_DIM), jnp.float32)
+
+    def call(kernel, c, outs, operands):
         return pl.pallas_call(
-            functools.partial(attend_kernel, c, last),
+            functools.partial(kernel, c),
             out_shape=outs,
             out_specs=(vmem, vmem),
-            in_specs=[smem] + [vmem] * (5 + len(rest)),
+            in_specs=[smem] + [vmem] * len(operands),
             compiler_params=small,
-            cost_estimate=pl.CostEstimate(flops=flops, bytes_accessed=tok * width * 20, transcendentals=3 * tok * tok * 2),
-        )(me1, queries, chunk[c], aux, x0, a0, *rest)
+            cost_estimate=cost,
+        )(me1, *operands)
 
     att, sq = [], []
     for c, (near, far) in enumerate(((x0, a0), (x1, a1), (x2, a2))):
-        o, q = attend(c, False, (near, far))
+        outs = (att_shape, jax.ShapeDtypeStruct((tok, HEAD_DIM), jnp.float32))
+        o, q = call(attend_kernel, c, outs, (queries, chunk[c], aux, x0, a0, near, far))
         att.append(o)
         sq.append(q)
-    o, q = attend(3, True, (s, f, a3, *sq))
+    c = CHUNKS - 1
+    state = call(partial_kernel, c, (acc_shape, stat_shape), (queries, chunk[c], aux, x0, a0, s, f))
+    outs = (att_shape, jax.ShapeDtypeStruct((8, tok), jnp.float32))
+    o, q = call(last_kernel, c, outs, (queries, aux, a0, a3, *state, *sq))
     att.append(o)
     tp = lax.axis_size("tp")
     other = lax.ppermute(q, "tp", [(i, i ^ 1) for i in range(tp)])

time: 42.2 us -> 39.5 us (0.936)
  the two profiles are of different devices: /device:TPU:11 before, /device:TPU:13 now
where the time goes in v4:
time: 39.5 us; the launch traced here: 39.3 us
  waiting for transfers between devices  15.8 us (40%)
  starting transfers between devices  14.7 us (37%)
  Pallas kernels  8.5 us (22%)
    ppermute x9, waiting for transfers between devices, send(): return lax.ppermute(value, 'seq', pairs)  15 us
    ppermute x9, starting transfers between devices, send(): return lax.ppermute(value, 'seq', pairs)  12.4 us
    pallas_call x5, Pallas kernels, call(): pl.pallas_call(functools.partial(kernel, c), out_shape=outs, out_specs=(v...  5.17 us
    ppermute x1, starting transfers between devices, on_device(): other = lax.ppermute(q, 'tp', [(i, i ^ 1) for i in range(tp)])  2.39 us
    pallas_call x1, Pallas kernels, on_device(): pl.pallas_call(pack_rest_kernel, out_shape=tuple((jax.ShapeDtypeStruct((t...  1.26 us
    pallas_call x1, Pallas kernels, on_device(): pl.pallas_call(pack_kernel, out_shape=(jax.ShapeDtypeStruct((tok + SEG_RO...  1.03 us
    pallas_call x1, Pallas kernels, on_device(): pl.pallas_call(functools.partial(finish_kernel, float(feat * tp)), out_sh...  1.03 us
    ppermute x1, waiting for transfers between devices, on_device(): other = lax.ppermute(q, 'tp', [(i, i ^ 1) for i in range(tp)])  0.83 us
  transfers between devices with their start and end apart: 10, of which 6 were waited for; matrix products, arithmetic and copies ran while one was open for 0% of the time, Pallas kernels for 14%

profile of v4, /device:TPU:13, one launch (start us, length us, event | category | flops | bytes accessed | tf_op | source)
XLA Modules:
  0.0 39.3 jit_solution(220285581767759058)
XLA Ops:
  0.0 1.3 %pack_rest.1 = (bf16[256,512]{1,0:T(8,128)(2,1)S(1)}, bf16[256,512]{1,0:T(8,128)(2,1)S(1)}, bf16[256,512]{1,0:T(8,128)(2,1)S(1)}) custom-call(bf16[256,1024]{1,0:T(8,128)(2,1)} %keys_ref.3, bf16[256,1024]{1,0:T(8,128)(2,1)} %values_ref.3), custom_call_target="tpu_custom_call" | custom-call | tf_op jit(solution)/shard_map/pack_rest/pallas_call | solution.py:266
  1.3 1.3 %collective-permute-start.5 = (bf16[256,512]{1,0:T(8,128)(2,1)S(1)}, bf16[256,512]{1,0:T(8,128)(2,1)S(1)}, u32[]{:S(2)}, u32[]{:S(2)}) collective-permute-start(bf16[256,512]{1,0:T(8,128)(2,1)S(1)} %get-tuple-element.26.own_ref), channel_id=1, source_target_pairs={{0,4},{2,6},{4,8},{6,10},{8,12},{10,14},{12,0},{14,2},{1,5},{3,7},... | collective-permute-start | bytes 786440 | tf_op jit(solution)/shard_map/ppermute | solution.py:243
  2.6 1.3 %collective-permute-start.7 = (bf16[256,512]{1,0:T(8,128)(2,1)S(1)}, bf16[256,512]{1,0:T(8,128)(2,1)S(1)}, u32[]{:S(2)}, u32[]{:S(2)}) collective-permute-start(bf16[256,512]{1,0:T(8,128)(2,1)S(1)} %get-tuple-element.28.own_ref), channel_id=1, source_target_pairs={{0,4},{2,6},{4,8},{6,10},{8,12},{10,14},{12,0},{14,2},{1,5},{3,7},... | collective-permute-start | bytes 786440 | tf_op jit(solution)/shard_map/ppermute | solution.py:243
  3.9 1.0 %pack.1 = (bf16[272,512]{1,0:T(8,128)(2,1)S(1)}, f32[8,256]{1,0:T(8,128)S(1)}) custom-call(s32[1]{0:T(128)} %bitcast.me_ref, bf16[256,1024]{1,0:T(8,128)(2,1)} %keys_ref.3, bf16[256,1024]{1,0:T(8,128)(2,1)} %values_ref.3, s32[1,256]{1,0:T(1,128)} %bitcast.3, s32[1,256]{1,0:T(1,128)} %bitcast.4), custom_call_target="tpu_custom_call" | custom-call | tf_op jit(solution)/shard_map/pack/pallas_call | solution.py:254
  5.0 0.1 collective-permute-start
  5.1 1.2 %collective-permute-start.3 = (bf16[256,512]{1,0:T(8,128)(2,1)S(1)}, bf16[256,512]{1,0:T(8,128)(2,1)S(1)}, u32[]{:S(2)}, u32[]{:S(2)}) collective-permute-start(bf16[256,512]{1,0:T(8,128)(2,1)S(1)} %get-tuple-element.22.own_ref), channel_id=1, source_target_pairs={{0,2},{2,0},{4,6},{6,4},{8,10},{10,8},{12,14},{14,12},{1,3},{3,1},... | collective-permute-start | bytes 786440 | tf_op jit(solution)/shard_map/ppermute | solution.py:243
  6.3 2.2 %collective-permute-done.5.far_ref = bf16[256,512]{1,0:T(8,128)(2,1)S(1)} collective-permute-done((bf16[256,512]{1,0:T(8,128)(2,1)S(1)}, bf16[256,512]{1,0:T(8,128)(2,1)S(1)}, u32[]{:S(2)}, u32[]{:S(2)}) %collective-permute-start.5) | collective-permute-done | bytes 262176 | tf_op jit(solution)/shard_map/ppermute | solution.py:243
  8.5 1.3 %collective-permute-start.6 = (bf16[256,512]{1,0:T(8,128)(2,1)S(1)}, bf16[256,512]{1,0:T(8,128)(2,1)S(1)}, u32[]{:S(2)}, u32[]{:S(2)}) collective-permute-start(bf16[256,512]{1,0:T(8,128)(2,1)S(1)} %broadcast_select_fusion.2), channel_id=1, source_target_pairs={{0,2},{2,0},{4,6},{6,4},{8,10},{10,8},{12,14},{14,12},{1,3},{3,1},... | collective-permute-start | bytes 786440 | tf_op jit(solution)/shard_map/ppermute | solution.py:243
  9.8 4.3 %collective-permute-done.7.far_ref = bf16[256,512]{1,0:T(8,128)(2,1)S(1)} collective-permute-done((bf16[256,512]{1,0:T(8,128)(2,1)S(1)}, bf16[256,512]{1,0:T(8,128)(2,1)S(1)}, u32[]{:S(2)}, u32[]{:S(2)}) %collective-permute-start.7) | collective-permute-done | bytes 262176 | tf_op jit(solution)/shard_map/ppermute | solution.py:243
  14.2 1.3 %collective-permute-start.8 = (bf16[256,512]{1,0:T(8,128)(2,1)S(1)}, bf16[256,512]{1,0:T(8,128)(2,1)S(1)}, u32[]{:S(2)}, u32[]{:S(2)}) collective-permute-start(bf16[256,512]{1,0:T(8,128)(2,1)S(1)} %broadcast_select_fusion.1), channel_id=1, source_target_pairs={{0,2},{2,0},{4,6},{6,4},{8,10},{10,8},{12,14},{14,12},{1,3},{3,1},... | collective-permute-start | bytes 786440 | tf_op jit(solution)/shard_map/ppermute | solution.py:243
  15.4 4.7 %collective-permute-done.far_seg_ref.far_ref = bf16[272,512]{1,0:T(8,128)(2,1)S(1)} collective-permute-done((bf16[272,512]{1,0:T(8,128)(2,1)S(1)}, bf16[272,512]{1,0:T(8,128)(2,1)S(1)}, u32[]{:S(2)}, u32[]{:S(2)}) %collective-permute-start) | collective-permute-done | bytes 278560 | tf_op jit(solution)/shard_map/ppermute | solution.py:243
  20.1 0.0 copy-start
  20.1 1.3 %collective-permute-start.2 = (bf16[272,512]{1,0:T(8,128)(2,1)S(1)}, bf16[272,512]{1,0:T(8,128)(2,1)S(1)}, u32[]{:S(2)}, u32[]{:S(2)}) collective-permute-start(bf16[272,512]{1,0:T(8,128)(2,1)S(1)} %broadcast_select_fusion), channel_id=1, source_target_pairs={{0,2},{2,0},{4,6},{6,4},{8,10},{10,8},{12,14},{14,12},{1,3},{3,1},... | collective-permute-start | bytes 835592 | tf_op jit(solution)/shard_map/ppermute | solution.py:243
  21.4 0.0 collective-permute-done.3.s_ref
  21.5 1.3 %collective-permute-start.4 = (bf16[256,512]{1,0:T(8,128)(2,1)S(1)}, bf16[256,512]{1,0:T(8,128)(2,1)S(1)}, u32[]{:S(2)}, u32[]{:S(2)}) collective-permute-start(bf16[256,512]{1,0:T(8,128)(2,1)S(1)} %broadcast_select_fusion.3), channel_id=1, source_target_pairs={{0,4},{2,6},{4,8},{6,10},{8,12},{10,14},{12,0},{14,2},{1,5},{3,7},... | collective-permute-start | bytes 786440 | tf_op jit(solution)/shard_map/ppermute | solution.py:243
  22.8 3.2 %collective-permute-start.1 = (bf16[256,512]{1,0:T(8,128)(2,1)S(1)}, bf16[256,512]{1,0:T(8,128)(2,1)S(1)}, u32[]{:S(2)}, u32[]{:S(2)}) collective-permute-start(bf16[256,512]{1,0:T(8,128)(2,1)S(1)} %get-tuple-element.22.own_ref), channel_id=1, source_target_pairs={{0,4},{2,6},{4,8},{6,10},{8,12},{10,14},{1,5},{3,7},{5,9},{7,11},{... | collective-permute-start | bytes 786440 | tf_op jit(solution)/shard_map/ppermute | solution.py:243
  26.0 2.9 %collective-permute-done.2.near_seg_ref.near_ref = bf16[272,512]{1,0:T(8,128)(2,1)S(1)} collective-permute-done((bf16[272,512]{1,0:T(8,128)(2,1)S(1)}, bf16[272,512]{1,0:T(8,128)(2,1)S(1)}, u32[]{:S(2)}, u32[]{:S(2)}) %collective-permute-start.2) | collective-permute-done | bytes 278560 | tf_op jit(solution)/shard_map/ppermute | solution.py:243
  28.9 0.0 copy-done
  28.9 1.1 %shard_map.65 = (bf16[256,256]{1,0:T(8,128)(2,1)S(1)}, f32[256,128]{1,0:T(8,128)S(1)}) custom-call(s32[1]{0:T(128)} %bitcast.me_ref, bf16[256,1024]{1,0:T(8,128)(2,1)S(1)} %copy-done, bf16[272,512]{1,0:T(8,128)(2,1)S(1)} %get-tuple-element.21.own_ref, f32[8,256]{1,0:T(8,128)S(1)} %get-tuple-element.20.aux_ref, ...), custom_call_target="tpu_custom_call" | custom-call | flops 201326592 | bytes 1310720 | tf_op jit(solution)/shard_map/pallas_call | solution.py:294
  30.0 0.0 collective-permute-done.6.near_ref
  30.0 1.2 %shard_map.66 = (bf16[256,256]{1,0:T(8,128)(2,1)S(1)}, f32[256,128]{1,0:T(8,128)S(1)}) custom-call(s32[1]{0:T(128)} %bitcast.me_ref, bf16[256,1024]{1,0:T(8,128)(2,1)S(1)} %copy-done, bf16[256,512]{1,0:T(8,128)(2,1)S(1)} %get-tuple-element.26.own_ref, f32[8,256]{1,0:T(8,128)S(1)} %get-tuple-element.20.aux_ref, ...), custom_call_target="tpu_custom_call" | custom-call | flops 201326592 | bytes 1310720 | tf_op jit(solution)/shard_map/pallas_call | solution.py:294
  31.2 0.0 collective-permute-done.8.near_ref
  31.2 1.1 %shard_map.67 = (bf16[256,256]{1,0:T(8,128)(2,1)S(1)}, f32[256,128]{1,0:T(8,128)S(1)}) custom-call(s32[1]{0:T(128)} %bitcast.me_ref, bf16[256,1024]{1,0:T(8,128)(2,1)S(1)} %copy-done, bf16[256,512]{1,0:T(8,128)(2,1)S(1)} %get-tuple-element.28.own_ref, f32[8,256]{1,0:T(8,128)S(1)} %get-tuple-element.20.aux_ref, ...), custom_call_target="tpu_custom_call" | custom-call | flops 201326592 | bytes 1310720 | tf_op jit(solution)/shard_map/pallas_call | solution.py:294
  32.4 0.0 collective-permute-done.4.f_ref
  32.4 0.9 %shard_map.64 = (f32[256,256]{1,0:T(8,128)S(1)}, f32[4,256,128]{2,1,0:T(8,128)S(1)}) custom-call(s32[1]{0:T(128)} %bitcast.me_ref, bf16[256,1024]{1,0:T(8,128)(2,1)S(1)} %copy-done, bf16[256,512]{1,0:T(8,128)(2,1)S(1)} %get-tuple-element.22.own_ref, f32[8,256]{1,0:T(8,128)S(1)} %get-tuple-element.20.aux_ref, ...), custom_call_target="tpu_custom_call" | custom-call | flops 201326592 | bytes 1310720 | tf_op jit(solution)/shard_map/pallas_call | solution.py:294
  33.3 0.9 %collective-permute-done.1.far_ref = bf16[256,512]{1,0:T(8,128)(2,1)S(1)} collective-permute-done((bf16[256,512]{1,0:T(8,128)(2,1)S(1)}, bf16[256,512]{1,0:T(8,128)(2,1)S(1)}, u32[]{:S(2)}, u32[]{:S(2)}) %collective-permute-start.1) | collective-permute-done | bytes 262176 | tf_op jit(solution)/shard_map/ppermute | solution.py:243
  34.2 0.8 %shard_map.68 = (bf16[256,256]{1,0:T(8,128)(2,1)S(1)}, f32[8,256]{1,0:T(8,128)S(1)}) custom-call(s32[1]{0:T(128)} %bitcast.me_ref, bf16[256,1024]{1,0:T(8,128)(2,1)S(1)} %copy-done, f32[8,256]{1,0:T(8,128)S(1)} %get-tuple-element.20.aux_ref, bf16[272,512]{1,0:T(8,128)(2,1)S(1)} %collective-permute-done.far_seg_ref.far_ref, ...), custom_call_target="tpu_custom_call" | custom-call | flops 201326592 | bytes 1310720 | tf_op jit(solution)/shard_map/pallas_call | solution.py:294
  35.0 0.0 copy-start.1
  35.0 2.4 %collective-permute-start.9 = (f32[8,256]{1,0:T(8,128)S(1)}, f32[8,256]{1,0:T(8,128)S(1)}, u32[]{:S(2)}, u32[]{:S(2)}) collective-permute-start(f32[8,256]{1,0:T(8,128)S(1)} %get-tuple-element.30.mine_ref), channel_id=1, source_target_pairs={{0,1},{1,0},{2,3},{3,2},{4,5},{5,4},{6,7},{7,6},{8,9},{9,8},{10,11... | collective-permute-start | bytes 24584 | tf_op jit(solution)/shard_map/ppermute | solution.py:315
  37.4 0.8 %collective-permute-done.9.other_ref = f32[8,256]{1,0:T(8,128)S(1)} collective-permute-done((f32[8,256]{1,0:T(8,128)S(1)}, f32[8,256]{1,0:T(8,128)S(1)}, u32[]{:S(2)}, u32[]{:S(2)}) %collective-permute-start.9) | collective-permute-done | bytes 8224 | tf_op jit(solution)/shard_map/ppermute | solution.py:315
  38.2 0.0 copy-done.1
  38.2 1.0 %finish.1 = bf16[256,1024]{1,0:T(8,128)(2,1)} custom-call(f32[8,256]{1,0:T(8,128)S(1)} %get-tuple-element.30.mine_ref, f32[8,256]{1,0:T(8,128)S(1)} %collective-permute-done.9.other_ref, f32[8,256]{1,0:T(8,128)S(1)} %get-tuple-element.20.aux_ref, f32[2,1024]{1,0:T(2,128)S(1)} %copy-done.1, bf16[256,256]{1,0:T(8,128)(2,1)S(1)} %get-tuple-element.31.refs_0_, ...), custom_call_target="tpu_custom_call" | custom-call | tf_op jit(solution)/shard_map/finish/pallas_call | solution.py:316
  (4 shorter events, 0.1 us)
Async XLA Ops:
  1.3 7.2 %collective-permute-start.5 = (bf16[256,512]{1,0:T(8,128)(2,1)S(1)}, bf16[256,512]{1,0:T(8,128)(2,1)S(1)}, u32[]{:S(2)}, u32[]{:S(2)}) collective-permute-start(bf16[256,512]{1,0:T(8,128)(2,1)S(1)} %get-tuple-element.26.own_ref), channel_id=1, source_target_pairs={{0,4},{2,6},{4,8},{6,10},{8,12},{10,14},{12,0},{14,2},{1,5},{3,7},... | collective-permute-start | bytes 786440 | tf_op jit(solution)/shard_map/ppermute | solution.py:243
  2.6 11.5 %collective-permute-start.7 = (bf16[256,512]{1,0:T(8,128)(2,1)S(1)}, bf16[256,512]{1,0:T(8,128)(2,1)S(1)}, u32[]{:S(2)}, u32[]{:S(2)}) collective-permute-start(bf16[256,512]{1,0:T(8,128)(2,1)S(1)} %get-tuple-element.28.own_ref), channel_id=1, source_target_pairs={{0,4},{2,6},{4,8},{6,10},{8,12},{10,14},{12,0},{14,2},{1,5},{3,7},... | collective-permute-start | bytes 786440 | tf_op jit(solution)/shard_map/ppermute | solution.py:243
  5.0 15.1 %collective-permute-start = (bf16[272,512]{1,0:T(8,128)(2,1)S(1)}, bf16[272,512]{1,0:T(8,128)(2,1)S(1)}, u32[]{:S(2)}, u32[]{:S(2)}) collective-permute-start(bf16[272,512]{1,0:T(8,128)(2,1)S(1)} %get-tuple-element.21.own_ref), channel_id=1, source_target_pairs={{0,4},{2,6},{4,8},{6,10},{8,12},{10,14},{12,0},{14,2},{1,5},{3,7},... | collective-permute-start | bytes 835592 | tf_op jit(solution)/shard_map/ppermute | solution.py:243
  5.1 16.3 %collective-permute-start.3 = (bf16[256,512]{1,0:T(8,128)(2,1)S(1)}, bf16[256,512]{1,0:T(8,128)(2,1)S(1)}, u32[]{:S(2)}, u32[]{:S(2)}) collective-permute-start(bf16[256,512]{1,0:T(8,128)(2,1)S(1)} %get-tuple-element.22.own_ref), channel_id=1, source_target_pairs={{0,2},{2,0},{4,6},{6,4},{8,10},{10,8},{12,14},{14,12},{1,3},{3,1},... | collective-permute-start | bytes 786440 | tf_op jit(solution)/shard_map/ppermute | solution.py:243
  8.5 21.5 %collective-permute-start.6 = (bf16[256,512]{1,0:T(8,128)(2,1)S(1)}, bf16[256,512]{1,0:T(8,128)(2,1)S(1)}, u32[]{:S(2)}, u32[]{:S(2)}) collective-permute-start(bf16[256,512]{1,0:T(8,128)(2,1)S(1)} %broadcast_select_fusion.2), channel_id=1, source_target_pairs={{0,2},{2,0},{4,6},{6,4},{8,10},{10,8},{12,14},{14,12},{1,3},{3,1},... | collective-permute-start | bytes 786440 | tf_op jit(solution)/shard_map/ppermute | solution.py:243
  14.2 17.0 %collective-permute-start.8 = (bf16[256,512]{1,0:T(8,128)(2,1)S(1)}, bf16[256,512]{1,0:T(8,128)(2,1)S(1)}, u32[]{:S(2)}, u32[]{:S(2)}) collective-permute-start(bf16[256,512]{1,0:T(8,128)(2,1)S(1)} %broadcast_select_fusion.1), channel_id=1, source_target_pairs={{0,2},{2,0},{4,6},{6,4},{8,10},{10,8},{12,14},{14,12},{1,3},{3,1},... | collective-permute-start | bytes 786440 | tf_op jit(solution)/shard_map/ppermute | solution.py:243
  20.1 8.8 %copy-start = (bf16[256,1024]{1,0:T(8,128)(2,1)S(1)}, bf16[256,1024]{1,0:T(8,128)(2,1)}, u32[]{:S(2)}) copy-start(bf16[256,1024]{1,0:T(8,128)(2,1)} %q_ref.9) | copy-start | bytes 1572868
  20.1 8.7 %collective-permute-start.2 = (bf16[272,512]{1,0:T(8,128)(2,1)S(1)}, bf16[272,512]{1,0:T(8,128)(2,1)S(1)}, u32[]{:S(2)}, u32[]{:S(2)}) collective-permute-start(bf16[272,512]{1,0:T(8,128)(2,1)S(1)} %broadcast_select_fusion), channel_id=1, source_target_pairs={{0,2},{2,0},{4,6},{6,4},{8,10},{10,8},{12,14},{14,12},{1,3},{3,1},... | collective-permute-start | bytes 835592 | tf_op jit(solution)/shard_map/ppermute | solution.py:243
  21.5 10.9 %collective-permute-start.4 = (bf16[256,512]{1,0:T(8,128)(2,1)S(1)}, bf16[256,512]{1,0:T(8,128)(2,1)S(1)}, u32[]{:S(2)}, u32[]{:S(2)}) collective-permute-start(bf16[256,512]{1,0:T(8,128)(2,1)S(1)} %broadcast_select_fusion.3), channel_id=1, source_target_pairs={{0,4},{2,6},{4,8},{6,10},{8,12},{10,14},{12,0},{14,2},{1,5},{3,7},... | collective-permute-start | bytes 786440 | tf_op jit(solution)/shard_map/ppermute | solution.py:243
  22.8 11.3 %collective-permute-start.1 = (bf16[256,512]{1,0:T(8,128)(2,1)S(1)}, bf16[256,512]{1,0:T(8,128)(2,1)S(1)}, u32[]{:S(2)}, u32[]{:S(2)}) collective-permute-start(bf16[256,512]{1,0:T(8,128)(2,1)S(1)} %get-tuple-element.22.own_ref), channel_id=1, source_target_pairs={{0,4},{2,6},{4,8},{6,10},{8,12},{10,14},{1,5},{3,7},{5,9},{7,11},{... | collective-permute-start | bytes 786440 | tf_op jit(solution)/shard_map/ppermute | solution.py:243
  35.0 3.2 %copy-start.1 = (f32[2,1024]{1,0:T(2,128)S(1)}, f32[2,1024]{1,0:T(2,128)}, u32[]{:S(2)}) copy-start(f32[2,1024]{1,0:T(2,128)} %gain_ref.1) | copy-start | bytes 24580
  35.0 3.2 %collective-permute-start.9 = (f32[8,256]{1,0:T(8,128)S(1)}, f32[8,256]{1,0:T(8,128)S(1)}, u32[]{:S(2)}, u32[]{:S(2)}) collective-permute-start(f32[8,256]{1,0:T(8,128)S(1)} %get-tuple-element.30.mine_ref), channel_id=1, source_target_pairs={{0,1},{1,0},{2,3},{3,2},{4,5},{5,4},{6,7},{7,6},{8,9},{9,8},{10,11... | collective-permute-start | bytes 24584 | tf_op jit(solution)/shard_map/ppermute | solution.py:315
